TPU v7x, 512 devices: a whole 4x4x16 slice. The times are simulated.
512 devices in a mesh: dp: 8 (over x, core), expert: 64 (over y, z).
Axes of the slice: x: 4, y: 4, z: 16, core: 2. Of those that a mesh axis runs over, the one named last changes fastest.
Arguments:
- tokens: bfloat16 [8192, 2048], P('expert', 'dp'), may hold values from -6 to 6
- cotangent: bfloat16 [8192, 2048], P('expert', 'dp'), may hold values from -6 to 6
- routes: int32 [8192, 8], P('expert'), may hold values from 0 to 63, as said below
- mix_weights: float32 [8192, 8], P('expert'), may hold values from 0.05 to 0.5
- w_gate: bfloat16 [64, 2048, 384], P('expert', 'dp'), may hold values from -0.125 to 0.125
- w_up: bfloat16 [64, 2048, 384], P('expert', 'dp'), may hold values from -0.125 to 0.125
- w_down: bfloat16 [64, 384, 2048], P('expert', None, 'dp'), may hold values from -0.3125 to 0.3125
Outputs:
- mixed: bfloat16 [8192, 2048], P('expert', 'dp')
- token_grad: bfloat16 [8192, 2048], P('expert', 'dp')
- gate_grad: float32 [64, 2048, 384], P('expert', 'dp')
- up_grad: float32 [64, 2048, 384], P('expert', 'dp')
- down_grad: float32 [64, 384, 2048], P('expert', None, 'dp')
Inputs may be any that keep to these rules, and one draw needn't show every extreme that they name: `routes`: each row names 8 different experts. In each aligned block of 128 rows at most 32 rows name the same expert, and some block reaches that. In all, at most 1792 rows name one expert, and some expert is named by exactly that many.
All inputs are finite; a program needn't handle non-finite values.
Results may differ from a plain program's by a relative error of at most 0.023.
Values may be sent and summed in bfloat16 or wider, within the bound.
A program may use at most 64 MiB of HBM per device.

v0:
```python
import jax
import jax.numpy as jnp
from jax import lax
from jax.sharding import PartitionSpec as P


def contract(left_side, right_side, left_dim, right_dim):
    return lax.dot_general(
        left_side,
        right_side,
        (((left_dim,), (right_dim,)), ((), ())),
        preferred_element_type=jnp.float32,
    )


def silu_parts(gate_in):
    logistic = jax.nn.sigmoid(gate_in)
    return (gate_in * logistic, logistic * (1.0 + gate_in * (1.0 - logistic)))


def shards(tokens, cotangent, routes, mix_weights, w_gate, w_up, w_down):
    tok_rows, width_dev = tokens.shape
    picks_per = routes.shape[1]
    owner_count = lax.axis_size("expert")
    send_cap = 2 * tok_rows * picks_per // owner_count
    expert_cap = 7 * tok_rows * picks_per // 4
    slot_total = owner_count * send_cap
    gate_matrix = w_gate[0]
    up_matrix = w_up[0]
    down_matrix = w_down[0]
    flat_routes = routes.reshape(-1)
    owner_ids = jnp.arange(owner_count, dtype=jnp.int32)
    onehot = (owner_ids[:, None] == flat_routes[None, :]).astype(jnp.int32)
    earlier = jnp.cumsum(onehot, axis=1) - onehot
    rank_in = jnp.sum(earlier * onehot, axis=0)
    slot_index = flat_routes * send_cap + rank_in
    sent_counts = jnp.sum(onehot, axis=1).reshape(owner_count, 1)

    def to_slots(values):
        empty_rows = jnp.zeros((slot_total, width_dev), values.dtype)
        return empty_rows.at[slot_index].set(values).reshape(owner_count, send_cap, width_dev)

    x_slots = to_slots(jnp.repeat(tokens, picks_per, axis=0))
    scaled = mix_weights[:, :, None] * cotangent[:, None, :].astype(jnp.float32)
    grad_slots = to_slots(scaled.astype(jnp.bfloat16).reshape(tok_rows * picks_per, width_dev))
    got_tokens, got_counts = (
        lax.all_to_all(x_slots, "expert", split_axis=0, concat_axis=0, tiled=True),
        lax.all_to_all(sent_counts, "expert", split_axis=0, concat_axis=0, tiled=True),
    )
    counts = got_counts[:, 0]
    starts = jnp.cumsum(counts) - counts
    position = jnp.arange(send_cap, dtype=jnp.int32)
    target = jnp.where(
        position[None, :] < counts[:, None], starts[:, None] + position[None, :], expert_cap
    ).reshape(-1)
    fetch_row = jnp.minimum(target, expert_cap - 1)

    def pack_rows(slot_rows):
        empty_rows = jnp.zeros((expert_cap, width_dev), slot_rows.dtype)
        return empty_rows.at[target].set(slot_rows.reshape(slot_total, width_dev), mode="drop")

    def unpack(rows_in):
        return rows_in[fetch_row].reshape(owner_count, send_cap, width_dev)

    packed_x = pack_rows(got_tokens)
    gate_part = jnp.dot(packed_x, gate_matrix, preferred_element_type=jnp.float32)
    up_part = jnp.dot(packed_x, up_matrix, preferred_element_type=jnp.float32)
    gate_in, up_in = (
        lax.psum(gate_part.astype(jnp.bfloat16), "dp").astype(jnp.float32),
        lax.psum(up_part.astype(jnp.bfloat16), "dp").astype(jnp.float32),
    )
    activated, slope_silu = silu_parts(gate_in)
    hidden_act = (activated * up_in).astype(jnp.bfloat16)
    expert_out = jnp.dot(hidden_act, down_matrix, preferred_element_type=jnp.float32).astype(
        jnp.bfloat16
    )
    back_out = lax.all_to_all(unpack(expert_out), "expert", split_axis=0, concat_axis=0, tiled=True)
    got_grad = lax.all_to_all(grad_slots, "expert", split_axis=0, concat_axis=0, tiled=True)
    packed_grad = pack_rows(got_grad)
    back_hidden = lax.psum(
        contract(packed_grad, down_matrix, 1, 1).astype(jnp.bfloat16), "dp"
    ).astype(jnp.float32)
    gate_back = (back_hidden * up_in * slope_silu).astype(jnp.bfloat16)
    up_back = (back_hidden * activated).astype(jnp.bfloat16)
    row_grad = (contract(gate_back, gate_matrix, 1, 1) + contract(up_back, up_matrix, 1, 1)).astype(
        jnp.bfloat16
    )
    gate_grad = contract(packed_x, gate_back, 0, 0)
    up_grad = contract(packed_x, up_back, 0, 0)
    down_grad = contract(hidden_act, packed_grad, 0, 0)
    back_grad = lax.all_to_all(unpack(row_grad), "expert", split_axis=0, concat_axis=0, tiled=True)

    def collect(returned):
        picked = returned.reshape(slot_total, width_dev)[slot_index]
        return picked.reshape(tok_rows, picks_per, width_dev).astype(jnp.float32)

    mixed = jnp.sum(mix_weights[:, :, None] * collect(back_out), axis=1).astype(jnp.bfloat16)
    token_grad = jnp.sum(collect(back_grad), axis=1).astype(jnp.bfloat16)
    return (mixed, token_grad, gate_grad[None], up_grad[None], down_grad[None])


def solution(mesh):
    placed = (
        P("expert", "dp"),
        P("expert", "dp"),
        P("expert", None),
        P("expert", None),
        P("expert", "dp", None),
        P("expert", "dp", None),
        P("expert", None, "dp"),
    )
    return jax.shard_map(
        shards,
        mesh=mesh,
        in_specs=placed,
        out_specs=(
            P("expert", "dp"),
            P("expert", "dp"),
            P("expert", "dp", None),
            P("expert", "dp", None),
            P("expert", None, "dp"),
        ),
        check_vma=False,
    )
```

profile of v0, /device:TPU:1, one launch (start us, length us, event | category | flops | bytes accessed | tf_op | source)
XLA Modules:
  0.0 427.6 jit_solution(10336787646805802478)
XLA Ops:
  7.2 0.8 copy.41
  8.3 0.7 copy.42
  9.0 19.3 %all-to-all-start = ((s32[64,1,1]{2,1,0:T(1,128)}), s32[64,1,1]{2,1,0:T(1,128)S(1)}, u32[]{:S(2)}, u32[]{:S(2)}) async-start(s32[64,1,1]{2,1,0:T(1,128)} %copy.42), calls=%async_computation | async-start | bytes 65536 | tf_op jit(solution)/shard_map/all_to_all | solution.py:48
  29.3 18.0 %reduce-window.19 = s32[64,8,128]{2,1,0:T(8,128)S(1)} reduce-window(s32[64,8,128]{2,1,0:T(8,128)S(1)} %fusion.25, s32[]{:T(128)} %constant.9.clone.1), window={size=1x1x128 pad=0_0x0_0x127_0}, to_apply=%region_2.3 | reduce-window | flops 8323072 | bytes 524292 | tf_op jit(solution)/shard_map/reduce-window.1
  48.1 6.5 %scatter_custom_fusion.2 = bf16[2048,256]{1,0:T(8,128)(2,1)} fusion(s32[1024]{0:T(1024)S(1)} %bitcast.75, f32[128,256]{1,0:T(8,128)S(1)} %convert_element_type.70, f32[1024]{0:T(1024)S(1)} %mul.74, bf16[]{:T(256)} %constant.8.clone.1), kind=kCustom, calls=%fused_computation.36 | custom fusion | flops 524288 | bytes 1183746 | tf_op jit(solution)/shard_map/scatter | solution.py:41
  54.6 14.6 %all-to-all-start.3 = ((bf16[64,32,256]{2,1,0:T(8,128)(2,1)}), bf16[64,32,256]{2,1,0:T(8,128)(2,1)S(1)}, u32[]{:S(2)}, u32[]{:S(2)}) async-start(bf16[64,32,256]{2,1,0:T(8,128)(2,1)} %bitcast.17), calls=%async_computation.3 | async-start | bytes 2097152 | tf_op jit(solution)/shard_map/all_to_all | solution.py:78
  69.2 6.0 %scatter_custom_fusion = bf16[2048,256]{1,0:T(8,128)(2,1)} fusion(s32[1024]{0:T(1024)S(1)} %bitcast.76, bf16[]{:T(256)} %constant.8.clone.1, bf16[128,256]{1,0:T(8,128)(2,1)S(1)} %copy-done.15), kind=kCustom, calls=%fused_computation.38 | custom fusion | bytes 1114114 | tf_op jit(solution)/shard_map/scatter | solution.py:41
  75.3 43.8 %all-to-all-done.3 = bf16[64,32,256]{2,1,0:T(8,128)(2,1)S(1)} async-done(((bf16[64,32,256]{2,1,0:T(8,128)(2,1)}), bf16[64,32,256]{2,1,0:T(8,128)(2,1)S(1)}, u32[]{:S(2)}, u32[]{:S(2)}) %all-to-all-start.3) | async-done | bytes 1048608 | tf_op jit(solution)/shard_map/all_to_all | solution.py:78
  119.1 10.6 %all-to-all-start.1 = ((bf16[64,32,256]{2,1,0:T(8,128)(2,1)}), bf16[64,32,256]{2,1,0:T(8,128)(2,1)S(1)}, u32[]{:S(2)}, u32[]{:S(2)}) async-start(bf16[64,32,256]{2,1,0:T(8,128)(2,1)} %bitcast.7), calls=%async_computation.1 | async-start | bytes 2097152 | tf_op jit(solution)/shard_map/all_to_all | solution.py:47
  130.1 1.2 reduce.2
  131.6 9.5 %scatter_custom_fusion.3 = bf16[1792,256]{1,0:T(8,128)(2,1)S(1)} fusion(s32[2048]{0:T(1024)S(1)} %bitcast.78, bf16[2048,256]{1,0:T(8,128)(2,1)S(1)} %bitcast.69, bf16[]{:T(256)} %constant.8.clone.1), kind=kCustom, calls=%fused_computation.44 | custom fusion | bytes 917506 | tf_op jit(solution)/shard_map/scatter | solution.py:60
  141.1 39.0 %all-to-all-done.1 = bf16[64,32,256]{2,1,0:T(8,128)(2,1)S(1)} async-done(((bf16[64,32,256]{2,1,0:T(8,128)(2,1)}), bf16[64,32,256]{2,1,0:T(8,128)(2,1)S(1)}, u32[]{:S(2)}, u32[]{:S(2)}) %all-to-all-start.1) | async-done | bytes 1048608 | tf_op jit(solution)/shard_map/all_to_all | solution.py:47
  180.1 9.5 %scatter_custom_fusion.1 = bf16[1792,256]{1,0:T(8,128)(2,1)S(1)} fusion(s32[2048]{0:T(1024)S(1)} %bitcast.79, bf16[2048,256]{1,0:T(8,128)(2,1)S(1)} %bitcast.70, bf16[]{:T(256)} %constant.8.clone.1), kind=kCustom, calls=%fused_computation.46 | custom fusion | bytes 917506 | tf_op jit(solution)/shard_map/scatter | solution.py:60
  189.7 1.7 convolution_convert_fusion.1
  191.4 1.8 convolution_convert_fusion.2
  193.1 1.7 convolution_convert_fusion
  194.9 82.3 %all-reduce.3.cloned.1.call-done = (bf16[1792,384]{1,0:T(8,128)(2,1)}, bf16[1792,384]{1,0:T(8,128)(2,1)}, bf16[1792,384]{1,0:T(8,128)(2,1)}) async-done(((bf16[1792,384]{1,0:T(8,128)(2,1)}, bf16[1792,384]{1,0:T(8,128)(2,1)}, bf16[1792,384]{1,0:T(8,128)(2,1)}), (bf16[1792,384]{1,0:T(8,128)(2,1)}, bf16[1792,384]{1,0:T(8,128)(2,1)}, bf16[1792,384]{1,0:T(8,128)(2,1)})) %all-reduce.3.cloned.1.call-update) | async-done | bytes 4128784 | tf_op jit(solution)/shard_map/psum | solution.py:70
  277.3 3.9 fusion.3
  283.3 9.0 %gather_fusion.2 = bf16[2048,256]{1,0:T(8,128)(2,1)} fusion(bf16[1792,256]{1,0:T(8,128)(2,1)S(1)} %fusion.9, s32[2048]{0:T(1024)S(1)} %broadcast_clamp_fusion), kind=kCustom, calls=%fused_computation.2 | custom fusion | bytes 2105344 | tf_op jit(solution)/shard_map/gather | solution.py:63
  292.3 15.4 %all-to-all-start.4 = ((bf16[64,32,256]{2,1,0:T(8,128)(2,1)}), bf16[64,32,256]{2,1,0:T(8,128)(2,1)S(1)}, u32[]{:S(2)}, u32[]{:S(2)}) async-start(bf16[64,32,256]{2,1,0:T(8,128)(2,1)} %bitcast.68), calls=%async_computation.4 | async-start | bytes 2097152 | tf_op jit(solution)/shard_map/all_to_all | solution.py:91
  307.7 1.6 convolution_convert_fusion.3
  309.3 9.0 %gather_fusion = bf16[2048,256]{1,0:T(8,128)(2,1)} fusion(bf16[1792,256]{1,0:T(8,128)(2,1)S(1)} %convolution_convert_fusion.3, s32[2048]{0:T(1024)S(1)} %broadcast_clamp_fusion), kind=kCustom, calls=%fused_computation | custom fusion | bytes 2105344 | tf_op jit(solution)/shard_map/gather | solution.py:63
  318.2 38.1 %all-to-all-done.4 = bf16[64,32,256]{2,1,0:T(8,128)(2,1)S(1)} async-done(((bf16[64,32,256]{2,1,0:T(8,128)(2,1)}), bf16[64,32,256]{2,1,0:T(8,128)(2,1)S(1)}, u32[]{:S(2)}, u32[]{:S(2)}) %all-to-all-start.4) | async-done | bytes 1048608 | tf_op jit(solution)/shard_map/all_to_all | solution.py:91
  356.4 10.8 %all-to-all-start.2 = ((bf16[64,32,256]{2,1,0:T(8,128)(2,1)}), bf16[64,32,256]{2,1,0:T(8,128)(2,1)S(1)}, u32[]{:S(2)}, u32[]{:S(2)}) async-start(bf16[64,32,256]{2,1,0:T(8,128)(2,1)} %bitcast.67), calls=%async_computation.2 | async-start | bytes 2097152 | tf_op jit(solution)/shard_map/all_to_all | solution.py:77
  367.2 2.9 convolution_bitcast_fusion.1
  370.1 1.4 convolution_bitcast_fusion.2
  371.7 1.3 convolution_bitcast_fusion
  373.0 3.9 gather_fusion.3
  377.0 1.0 bitcast_reduce_fusion
  377.9 37.9 %all-to-all-done.2 = bf16[64,32,256]{2,1,0:T(8,128)(2,1)S(1)} async-done(((bf16[64,32,256]{2,1,0:T(8,128)(2,1)}), bf16[64,32,256]{2,1,0:T(8,128)(2,1)S(1)}, u32[]{:S(2)}, u32[]{:S(2)}) %all-to-all-start.2) | async-done | bytes 1048608 | tf_op jit(solution)/shard_map/all_to_all | solution.py:77
  415.8 3.9 gather_fusion.1
  419.8 1.0 fusion.10
  (64 shorter events, 5.0 us)
Async XLA Ops:
  7.2 184.2 %copy-start = (bf16[1,256,384]{2,1,0:T(8,128)(2,1)S(1)}, bf16[1,256,384]{2,1,0:T(8,128)(2,1)}, u32[]{:S(2)}) copy-start(bf16[1,256,384]{2,1,0:T(8,128)(2,1)} %param.11) | copy-start | bytes 589828
  7.2 40.7 %copy-start.16 = (f32[128,8]{0,1:T(8,128)S(1)}, f32[128,8]{0,1:T(8,128)}, u32[]{:S(2)}) copy-start(f32[128,8]{0,1:T(8,128)} %param.10) | copy-start | bytes 12292
  7.2 40.9 %copy-start.14 = (bf16[128,256]{1,0:T(8,128)(2,1)S(1)}, bf16[128,256]{1,0:T(8,128)(2,1)}, u32[]{:S(2)}) copy-start(bf16[128,256]{1,0:T(8,128)(2,1)} %param.8) | copy-start | bytes 196612
  9.0 45.7 %all-to-all-start = ((s32[64,1,1]{2,1,0:T(1,128)}), s32[64,1,1]{2,1,0:T(1,128)S(1)}, u32[]{:S(2)}, u32[]{:S(2)}) async-start(s32[64,1,1]{2,1,0:T(1,128)} %copy.42), calls=%async_computation | async-start | bytes 65536 | tf_op jit(solution)/shard_map/all_to_all | solution.py:48
  48.0 6.7 %copy-start.12 = (f32[128,8]{1,0:T(8,128)}, f32[128,8]{1,0:T(8,128)S(1)}, u32[]{:S(2)}) copy-start(f32[128,8]{1,0:T(8,128)S(1)} %copy.40) | copy-start | bytes 12292
  48.1 21.1 %copy-start.15 = (bf16[128,256]{1,0:T(8,128)(2,1)S(1)}, bf16[128,256]{1,0:T(8,128)(2,1)}, u32[]{:S(2)}) copy-start(bf16[128,256]{1,0:T(8,128)(2,1)} %param.7) | copy-start | bytes 196612
  54.6 64.5 %all-to-all-start.3 = ((bf16[64,32,256]{2,1,0:T(8,128)(2,1)}), bf16[64,32,256]{2,1,0:T(8,128)(2,1)S(1)}, u32[]{:S(2)}, u32[]{:S(2)}) async-start(bf16[64,32,256]{2,1,0:T(8,128)(2,1)} %bitcast.17), calls=%async_computation.3 | async-start | bytes 2097152 | tf_op jit(solution)/shard_map/all_to_all | solution.py:78
  119.1 61.0 %all-to-all-start.1 = ((bf16[64,32,256]{2,1,0:T(8,128)(2,1)}), bf16[64,32,256]{2,1,0:T(8,128)(2,1)S(1)}, u32[]{:S(2)}, u32[]{:S(2)}) async-start(bf16[64,32,256]{2,1,0:T(8,128)(2,1)} %bitcast.7), calls=%async_computation.1 | async-start | bytes 2097152 | tf_op jit(solution)/shard_map/all_to_all | solution.py:47
  129.7 60.0 %copy-start.10 = (bf16[1,256,384]{2,1,0:T(8,128)(2,1)S(1)}, bf16[1,256,384]{2,1,0:T(8,128)(2,1)}, u32[]{:S(2)}) copy-start(bf16[1,256,384]{2,1,0:T(8,128)(2,1)} %param.12) | copy-start | bytes 589828
  129.7 147.6 %all-reduce.3.cloned.1.call-start = ((), (), s32[]{:S(2)}) async-start(), calls=%async_computation.5 | async-start | bytes 8257536 | tf_op jit(solution)/shard_map/psum | solution.py:70
  141.1 52.0 %copy-start.8 = (bf16[1792,256]{1,0:T(8,128)(2,1)}, bf16[1792,256]{1,0:T(8,128)(2,1)S(1)}, u32[]{:S(2)}) copy-start(bf16[1792,256]{1,0:T(8,128)(2,1)S(1)} %scatter_custom_fusion.3) | copy-start | bytes 2752516
  189.6 3.5 copy-start.1
  191.4 1.8 copy-start.11
  281.1 1.1 copy-start.3
  281.1 1.5 copy-start.5
  281.1 26.5 %copy-start.6 = (bf16[1792,384]{1,0:T(8,128)(2,1)}, bf16[1792,384]{1,0:T(8,128)(2,1)S(1)}, u32[]{:S(2)}) copy-start(bf16[1792,384]{1,0:T(8,128)(2,1)S(1)} %get-tuple-element.10) | copy-start | bytes 4128772
  292.3 64.1 %all-to-all-start.4 = ((bf16[64,32,256]{2,1,0:T(8,128)(2,1)}), bf16[64,32,256]{2,1,0:T(8,128)(2,1)S(1)}, u32[]{:S(2)}, u32[]{:S(2)}) async-start(bf16[64,32,256]{2,1,0:T(8,128)(2,1)} %bitcast.68), calls=%async_computation.4 | async-start | bytes 2097152 | tf_op jit(solution)/shard_map/all_to_all | solution.py:91
  318.2 49.0 %copy-start.2 = (bf16[1792,256]{1,0:T(8,128)(2,1)S(1)}, bf16[1792,256]{1,0:T(8,128)(2,1)}, u32[]{:S(2)}) copy-start(bf16[1792,256]{1,0:T(8,128)(2,1)} %copy-done.1) | copy-start | bytes 2752516
  356.4 59.4 %all-to-all-start.2 = ((bf16[64,32,256]{2,1,0:T(8,128)(2,1)}), bf16[64,32,256]{2,1,0:T(8,128)(2,1)S(1)}, u32[]{:S(2)}, u32[]{:S(2)}) async-start(bf16[64,32,256]{2,1,0:T(8,128)(2,1)} %bitcast.67), calls=%async_computation.2 | async-start | bytes 2097152 | tf_op jit(solution)/shard_map/all_to_all | solution.py:77
  367.2 2.9 copy-start.4
  370.1 1.4 copy-start.7
  370.1 1.6 copy-start.9
  415.8 3.9 copy-start.13
Sparse Core Ops, SparseCore 0:
  195.0 82.1 all-reduce.2
where the time goes:
time: 435 us; the launch traced here: 428 us
  waiting for transfers between devices  241 us (55%)
  starting transfers between devices  70.8 us (16%)
  local copies, waits for them, and re-layouts  54.5 us (13%)
  other arithmetic  33 us (8%)
  between operations  14.4 us (3%)
  matrix products  13.7 us (3%)
    psum x1, waiting for transfers between devices, shards(): lax.psum(up_part.astype(jnp.bfloat16), 'dp').astype(jnp.float32)  82.3 us
    all_to_all x1, waiting for transfers between devices, shards(): lax.all_to_all(grad_slots, 'expert', split_axis=0, concat_axis=0, tiled=T...  43.8 us
    all_to_all x1, waiting for transfers between devices, shards(): lax.all_to_all(x_slots, 'expert', split_axis=0, concat_axis=0, tiled=True)  39 us
    all_to_all x1, waiting for transfers between devices, shards(): lax.all_to_all(unpack(row_grad), 'expert', split_axis=0, concat_axis=0, t...  38.1 us
    all_to_all x1, waiting for transfers between devices, shards(): lax.all_to_all(unpack(expert_out), 'expert', split_axis=0, concat_axis=0,...  37.9 us
    all_to_all x1, starting transfers between devices, shards(): lax.all_to_all(sent_counts, 'expert', split_axis=0, concat_axis=0, tiled=...  19.3 us
    scatter x2, local copies, waits for them, and re-layouts, pack_rows(): empty_rows.at[target]  19 us
    another operation x4, other arithmetic  18.2 us
  transfers between devices with their start and end apart: 6, of which 5 were waited for; matrix products, arithmetic and copies ran while one was open for 15% of the time, Pallas kernels for 0%

commit v1 on v0

v1 whole, which is shorter than its diff:
```python
import jax
import jax.numpy as jnp
from jax import lax
from jax.sharding import PartitionSpec as P


def contract(left_side, right_side, left_dim, right_dim):
    return lax.dot_general(
        left_side,
        right_side,
        (((left_dim,), (right_dim,)), ((), ())),
        preferred_element_type=jnp.float32,
    )


def silu_parts(gate_in):
    logistic = jax.nn.sigmoid(gate_in)
    return (gate_in * logistic, logistic * (1.0 + gate_in * (1.0 - logistic)))


def split_three(values):
    high = values.astype(jnp.bfloat16)
    rest = values - high.astype(jnp.float32)
    middle = rest.astype(jnp.bfloat16)
    low = (rest - middle.astype(jnp.float32)).astype(jnp.bfloat16)
    return (high, middle, low)


def shards(tokens, cotangent, routes, mix_weights, w_gate, w_up, w_down):
    tok_rows, width_dev = tokens.shape
    picks_per = routes.shape[1]
    dp_count = lax.axis_size("dp")
    owner_count = lax.axis_size("expert")
    hidden = w_gate.shape[2]
    sub_rows = tok_rows // dp_count
    width = width_dev * dp_count
    me_dp = lax.axis_index("dp")
    me_expert = lax.axis_index("expert")

    weights_dev = jnp.concatenate([w_gate[0], w_up[0], w_down[0].T], axis=1)
    weights = lax.all_gather(weights_dev, "dp", axis=0, tiled=True)

    both = jnp.stack([tokens, cotangent]).reshape(2, dp_count, sub_rows, width_dev)
    both = lax.all_to_all(both, "dp", split_axis=1, concat_axis=1, tiled=True)
    both = both.transpose(2, 0, 1, 3).reshape(sub_rows, 2 * width)
    my_routes = lax.dynamic_slice_in_dim(routes, me_dp * sub_rows, sub_rows, 0)
    my_mix = lax.dynamic_slice_in_dim(mix_weights, me_dp * sub_rows, sub_rows, 0)
    extra = jnp.concatenate(
        [my_routes.astype(jnp.bfloat16), *split_three(my_mix)], axis=1
    )
    extra = jnp.pad(extra, ((0, 0), (0, 128 - extra.shape[1])))
    rows = lax.all_gather(
        jnp.concatenate([both, extra], axis=1), "expert", axis=0, tiled=True
    )
    x_rows = rows[:, :width]
    c_rows = rows[:, width : 2 * width]
    tail = rows[:, 2 * width : 2 * width + 4 * picks_per].astype(jnp.float32)
    tail = tail.reshape(-1, 4, picks_per)
    mix_all = tail[:, 1] + tail[:, 2] + tail[:, 3]
    named = tail[:, 0] == me_expert.astype(jnp.float32)
    weight_row = jnp.sum(jnp.where(named, mix_all, 0.0), axis=1, keepdims=True)

    w_in = weights[:, : 2 * hidden]
    w_out = weights[:, 2 * hidden :]
    pre = contract(x_rows, w_in, 1, 0)
    back_hidden = contract(c_rows, w_out, 1, 0) * weight_row
    gate_in, up_in = pre[:, :hidden], pre[:, hidden:]
    activated, slope_silu = silu_parts(gate_in)
    hidden_mix = (activated * up_in * weight_row).astype(jnp.bfloat16)
    gate_back = (back_hidden * up_in * slope_silu).astype(jnp.bfloat16)
    up_back = (back_hidden * activated).astype(jnp.bfloat16)
    in_back = jnp.concatenate([gate_back, up_back], axis=1)

    mixed_part = contract(hidden_mix, w_out, 1, 1).astype(jnp.bfloat16)
    grad_part = contract(in_back, w_in, 1, 1).astype(jnp.bfloat16)
    sums = lax.psum_scatter(
        jnp.concatenate([mixed_part, grad_part], axis=1),
        "expert",
        scatter_dimension=0,
        tiled=True,
    )
    in_grad = contract(x_rows, in_back, 0, 0).astype(jnp.bfloat16)
    out_grad = contract(c_rows, hidden_mix, 0, 0).astype(jnp.bfloat16)
    weight_grads = lax.psum_scatter(
        jnp.concatenate([in_grad, out_grad], axis=1), "dp", scatter_dimension=0, tiled=True
    ).astype(jnp.float32)
    sums = sums.reshape(sub_rows, 2, dp_count, width_dev).transpose(1, 2, 0, 3)
    sums = lax.all_to_all(sums, "dp", split_axis=1, concat_axis=1, tiled=True)
    sums = sums.reshape(2, tok_rows, width_dev)
    return (
        sums[0],
        sums[1],
        weight_grads[None, :, :hidden],
        weight_grads[None, :, hidden : 2 * hidden],
        weight_grads[:, 2 * hidden :].T[None],
    )


def solution(mesh):
    placed = (
        P("expert", "dp"),
        P("expert", "dp"),
        P("expert", None),
        P("expert", None),
        P("expert", "dp", None),
        P("expert", "dp", None),
        P("expert", None, "dp"),
    )
    return jax.shard_map(
        shards,
        mesh=mesh,
        in_specs=placed,
        out_specs=(
            P("expert", "dp"),
            P("expert", "dp"),
            P("expert", "dp", None),
            P("expert", "dp", None),
            P("expert", None, "dp"),
        ),
        check_vma=False,
    )
```

time: 435 us -> 1040 us (2.39)
  waiting for transfers between devices: 241 us -> 942 us
  starting transfers between devices: 70.8 us -> 25.4 us
  local copies, waits for them, and re-layouts: 54.5 us -> 10.1 us
  other arithmetic: 33 us -> 16.6 us
  matrix products: 13.7 us -> 29.7 us
    reduce_scatter x0 -> x2, waiting for transfers between devices: none -> 743 us  [the longest x1 718 us: shards(): lax.psum_scatter(jnp.concatenate([mixed_part, grad_part], axis=1), 'exper...]
    all_gather x0 -> x2, waiting for transfers between devices: none -> 193 us  [the longest x1 144 us: shards(): lax.all_gather(jnp.concatenate([both, extra], axis=1), 'expert', axis=0,...]
    all_to_all x5 -> x2, waiting for transfers between devices: 159 us -> 6.17 us  [the longest x1 3.57 us: shards(): both = lax.all_to_all(both, 'dp', split_axis=1, concat_axis=1, tiled=True)]
    psum x1 -> x0, waiting for transfers between devices: 82.3 us -> none  [shards(): lax.psum(up_part.astype(jnp.bfloat16), 'dp').astype(jnp.float32)]
    all_to_all x5 -> x2, starting transfers between devices: 70.6 us -> 25.1 us  [the longest x1 15 us: shards(): sums = lax.all_to_all(sums, 'dp', split_axis=1, concat_axis=1, tiled=True)]
    gather x4 -> x0, local copies, waits for them, and re-layouts: 25.8 us -> none  [the longest x2 18 us: unpack(): return rows_in[fetch_row].reshape(owner_count, send_cap, width_dev)]
    scatter x3 -> x0, local copies, waits for them, and re-layouts: 25.1 us -> none  [the longest x2 19 us: pack_rows(): empty_rows.at[target]]
    dot_general x6, matrix products: 8.68 us -> 29.7 us  [contract(): lax.dot_general(left_side, right_side, (((left_dim,), (right_dim,)), ((),...]
  transfers between devices with their start and end apart: 6 -> 6, of which waited for: 5 -> 6; matrix products, arithmetic and copies ran while one was open for 15% -> 3% of each run, Pallas kernels for 0% -> 0%
where the time goes in v1:
time: 1040 us
  waiting for transfers between devices  942 us (91%)
  matrix products  29.7 us (3%)
  starting transfers between devices  25.4 us (2%)
  other arithmetic  16.6 us (2%)
  between operations  13.9 us (1%)
    reduce_scatter x1, waiting for transfers between devices, shards(): lax.psum_scatter(jnp.concatenate([mixed_part, grad_part], axis=1), 'exper...  718 us
    all_gather x1, waiting for transfers between devices, shards(): lax.all_gather(jnp.concatenate([both, extra], axis=1), 'expert', axis=0,...  144 us
    all_gather x1, waiting for transfers between devices, shards(): weights = lax.all_gather(weights_dev, 'dp', axis=0, tiled=True)  49 us
    dot_general x6, matrix products, contract(): lax.dot_general(left_side, right_side, (((left_dim,), (right_dim,)), ((),...  29.7 us
    reduce_scatter x1, waiting for transfers between devices, shards(): lax.psum_scatter(jnp.concatenate([in_grad, out_grad], axis=1), 'dp', scat...  24.4 us
  transfers between devices with their start and end apart: 6, of which 6 were waited for; matrix products, arithmetic and copies ran while one was open for 3% of the time, Pallas kernels for 0%

profile of v1, /device:TPU:1, one launch (start us, length us, event | category | flops | bytes accessed | tf_op | source)
XLA Modules:
  0.0 1037.5 jit_solution(6336059974394394952)
XLA Ops:
  7.2 0.9 pad_maximum_fusion.6
  8.1 0.8 copy.61
  8.8 10.1 all-to-all-start
  19.0 0.8 subtract_convert_fusion
  19.8 0.8 dynamic-slice_convert_fusion
  20.7 3.6 all-to-all-done
  24.4 0.7 fusion.23
  25.1 1.1 copy.64
  26.2 1.1 copy.65
  27.2 1.8 pad_maximum_fusion.5
  29.1 143.9 %all-gather.3.cloned.1.call-done = bf16[1024,4224]{1,0:T(8,128)(2,1)} async-done(((bf16[16,4224]{1,0:T(8,128)(2,1)}), bf16[1024,4224]{1,0:T(8,128)(2,1)}) %all-gather.3.cloned.1.call-update) | async-done | bytes 8650768 | tf_op jit(solution)/shard_map/all_gather | solution.py:52
  173.1 1.0 slice.70
  174.2 49.0 %all-gather.5.cloned.1.call-done = bf16[2048,1152]{0,1:T(8,128)(2,1)} async-done(((bf16[256,1152]{0,1:T(8,128)(2,1)}), bf16[2048,1152]{0,1:T(8,128)(2,1)}) %all-gather.5.cloned.1.call-update) | async-done | bytes 4718608 | tf_op jit(solution)/shard_map/all_gather | solution.py:41
  223.2 6.3 fusion.6
  229.5 5.2 multiply_convert_fusion.1
  234.7 1.8 fusion.11
  236.5 3.6 fusion.8
  240.2 2.5 pad_maximum_fusion.1
  242.9 5.8 convolution_convert_fusion
  248.7 6.9 convolution_convert_fusion.1
  255.7 7.9 pad_maximum_fusion
  263.6 24.4 %reduce-scatter.5.cloned.1.call-done = bf16[256,1152]{0,1:T(8,128)(2,1)} async-done(((bf16[2048,1152]{0,1:T(8,128)(2,1)}), bf16[256,1152]{0,1:T(8,128)(2,1)}) %reduce-scatter.5.cloned.1.call-update) | async-done | bytes 589840 | tf_op jit(solution)/shard_map/reduce_scatter | solution.py:84
  288.1 1.1 convert_element_type.62
  289.2 718.3 %reduce-scatter.3.cloned.1.call-done = bf16[16,4096]{1,0:T(8,128)(2,1)} async-done(((bf16[1024,4096]{1,0:T(8,128)(2,1)}), bf16[16,4096]{1,0:T(8,128)(2,1)}) %reduce-scatter.3.cloned.1.call-update) | async-done | bytes 131088 | tf_op jit(solution)/shard_map/reduce_scatter | solution.py:76
  1007.5 0.9 copy.77
  1008.5 0.8 copy.79
  1009.2 15.0 %all-to-all-start.1 = ((bf16[2,8,16,256]{3,0,2,1:T(2,128)(2,1)}), bf16[2,8,16,256]{3,0,2,1:T(2,128)(2,1)S(1)}, u32[]{:S(2)}, u32[]{:S(2)}) async-start(bf16[2,8,16,256]{3,0,2,1:T(2,128)(2,1)} %bitcast.31), calls=%async_computation.2 | async-start | bytes 262144 | tf_op jit(solution)/shard_map/all_to_all | solution.py:88
  1024.2 0.8 slice_bitcast_fusion
  1025.1 0.9 copy.71
  1026.0 0.9 copy.70
  1026.9 2.6 all-to-all-done.1
  1029.7 0.6 copy.74
  (24 shorter events, 1.6 us)
Async XLA Ops:
  8.8 15.4 %all-to-all-start = ((bf16[2,8,16,256]{3,0,2,1:T(2,128)(2,1)}), bf16[2,8,16,256]{3,0,2,1:T(2,128)(2,1)S(1)}, u32[]{:S(2)}, u32[]{:S(2)}) async-start(bf16[2,8,16,256]{3,0,2,1:T(2,128)(2,1)} %copy.61), calls=%async_computation | async-start | bytes 262144 | tf_op jit(solution)/shard_map/all_to_all | solution.py:44
  19.0 154.1 %all-gather.3.cloned.1.call-start = ((), (), s32[]{:S(2)}) async-start(), calls=%async_computation.4 | async-start | bytes 8785920 | tf_op jit(solution)/shard_map/all_gather | solution.py:52
  25.0 198.1 %all-gather.5.cloned.1.call-start = ((), (), s32[]{:S(2)}) async-start(), calls=%async_computation.5 | async-start | bytes 5308416 | tf_op jit(solution)/shard_map/all_gather | solution.py:41
  29.1 259.0 %reduce-scatter.5.cloned.1.call-start = ((), (), s32[]{:S(2)}) async-start(), calls=%async_computation.7 | async-start | bytes 5308416 | tf_op jit(solution)/shard_map/reduce_scatter | solution.py:84
  223.2 11.5 %slice-start = ((s8[8650752]{0:T(1024)(128)(4,1)}), s8[4194304]{0:T(1024)(128)(4,1)S(1)}, s32[]{:S(2)}) async-start(s8[8650752]{0:T(1024)(128)(4,1)} %bitcast.44), calls=%async_computation.8 | async-start | bytes 8388608
  223.2 11.5 %slice-start.1 = ((s8[8650752]{0:T(1024)(128)(4,1)}), s8[4194304]{0:T(1024)(128)(4,1)S(1)}, s32[]{:S(2)}) async-start(s8[8650752]{0:T(1024)(128)(4,1)} %bitcast.44), calls=%async_computation.9 | async-start | bytes 8388608
  229.5 5.2 slice-start.2
  242.7 764.8 %reduce-scatter.3.cloned.1.call-start = ((), (), s32[]{:S(2)}) async-start(), calls=%async_computation.6 | async-start | bytes 8519680 | tf_op jit(solution)/shard_map/reduce_scatter | solution.py:76
  1009.2 20.3 %all-to-all-start.1 = ((bf16[2,8,16,256]{3,0,2,1:T(2,128)(2,1)}), bf16[2,8,16,256]{3,0,2,1:T(2,128)(2,1)S(1)}, u32[]{:S(2)}, u32[]{:S(2)}) async-start(bf16[2,8,16,256]{3,0,2,1:T(2,128)(2,1)} %bitcast.31), calls=%async_computation.2 | async-start | bytes 262144 | tf_op jit(solution)/shard_map/all_to_all | solution.py:88
Sparse Core Ops, SparseCore 0:
  25.2 147.8 all-gather.2
  175.2 47.9 all-gather.4
  242.8 45.1 reduce-scatter.4
  292.4 715.1 reduce-scatter.2

commit v2 on v1

--- a/solution.py
+++ b/solution.py
@@ -1,6 +1,10 @@
+import functools
+
 import jax
 import jax.numpy as jnp
 from jax import lax
+from jax.experimental import pallas as pl
+from jax.experimental.pallas import tpu as pltpu
 from jax.sharding import PartitionSpec as P
 
 
@@ -24,6 +28,226 @@
     middle = rest.astype(jnp.bfloat16)
     low = (rest - middle.astype(jnp.float32)).astype(jnp.bfloat16)
     return (high, middle, low)
+
+
+SIDE_Y = 4
+PIECES = 2
+
+
+def steps_of(count):
+    return (count // 2, count - 1 - count // 2)
+
+
+def ring_places(side_z):
+    me = lax.axis_index("expert")
+    y_at, z_at = me // side_z, lax.rem(me, side_z)
+
+    def along_z(offset):
+        return {"expert": y_at * side_z + lax.rem(z_at + offset + side_z, side_z)}
+
+    def along_y(offset):
+        return {"expert": lax.rem(y_at + offset + SIDE_Y, SIDE_Y) * side_z + z_at}
+
+    return (y_at, z_at, along_y, along_z)
+
+
+def greet(places):
+    barrier = pltpu.get_barrier_semaphore()
+    for place in places:
+        pl.semaphore_signal(
+            barrier, inc=1, device_id=place, device_id_type=pl.DeviceIdType.MESH
+        )
+    pl.semaphore_wait(barrier, len(places))
+
+
+def send(source, target, sems, place):
+    copy = pltpu.make_async_remote_copy(
+        src_ref=source,
+        dst_ref=target,
+        send_sem=sems[0],
+        recv_sem=sems[1],
+        device_id=place,
+        device_id_type=pl.DeviceIdType.MESH,
+    )
+    copy.start()
+    return copy
+
+
+def gather_kernel(side_z, own_ref, all_ref, y_send, y_recv, z_send, z_recv, own_sem):
+    y_at, z_at, along_y, along_z = ring_places(side_z)
+    own = pltpu.make_async_copy(own_ref, all_ref.at[y_at, z_at], own_sem)
+    own.start()
+    greet([along_y(1), along_y(-1), along_z(1), along_z(-1)])
+
+    def wrap(value, count):
+        return lax.rem(value + 2 * count, count)
+
+    sent = []
+    first = send(own_ref, all_ref.at[y_at, z_at], (y_send.at[0], y_recv.at[0]), along_y(1))
+    other = send(own_ref, all_ref.at[y_at, z_at], (y_send.at[1], y_recv.at[1]), along_y(-1))
+    first.wait_recv()
+    below = wrap(y_at - 1, SIDE_Y)
+    second = send(
+        all_ref.at[below, z_at], all_ref.at[below, z_at], (y_send.at[2], y_recv.at[2]), along_y(1)
+    )
+    other.wait_recv()
+    second.wait_recv()
+    own.wait()
+    sent += [first, other, second]
+    step_counts = steps_of(side_z)
+    span = SIDE_Y // PIECES
+    going = {}
+
+    def start(way, step, piece):
+        sign = 1 - 2 * way
+        block = all_ref.at[pl.ds(piece * span, span), wrap(z_at - sign * step, side_z)]
+        at = (way, step, piece)
+        going[at] = send(block, block, (z_send.at[at], z_recv.at[at]), along_z(sign))
+
+    for piece in range(PIECES):
+        for way in range(2):
+            start(way, 0, piece)
+    for step in range(step_counts[0]):
+        for piece in range(PIECES):
+            for way in range(2):
+                if step < step_counts[way]:
+                    going[(way, step, piece)].wait_recv()
+                    if step + 1 < step_counts[way]:
+                        start(way, step + 1, piece)
+    for copy in sent + list(going.values()):
+        copy.wait_send()
+
+
+def gather_rows(own, side_z):
+    rows, columns = own.shape
+    longest = steps_of(side_z)[0]
+    gathered = pl.pallas_call(
+        functools.partial(gather_kernel, side_z),
+        out_shape=jax.ShapeDtypeStruct((SIDE_Y, side_z, rows, columns), own.dtype),
+        in_specs=[pl.BlockSpec(memory_space=pltpu.VMEM)],
+        out_specs=pl.BlockSpec(memory_space=pltpu.VMEM),
+        scratch_shapes=[
+            pltpu.SemaphoreType.DMA((3,)),
+            pltpu.SemaphoreType.DMA((3,)),
+            pltpu.SemaphoreType.DMA((2, longest, PIECES)),
+            pltpu.SemaphoreType.DMA((2, longest, PIECES)),
+            pltpu.SemaphoreType.DMA,
+        ],
+        compiler_params=pltpu.CompilerParams(
+            collective_id=0, has_side_effects=True, vmem_limit_bytes=24 * 2**20
+        ),
+        cost_estimate=pl.CostEstimate(
+            flops=0, bytes_accessed=200 * 2**20, transcendentals=0
+        ),
+    )(own)
+    return gathered.reshape(-1, columns)
+
+
+def scatter_kernel(side_z, part_ref, sum_ref, got_up, got_down, y_held, y_got,
+                   z_send, z_recv, y_send, y_recv):
+    y_at, z_at, along_y, along_z = ring_places(side_z)
+    greet([along_y(1), along_y(-1), along_z(1), along_z(-1)])
+
+    def wrap(value, count):
+        return lax.rem(value + 2 * count, count)
+
+    step_counts = steps_of(side_z)
+    span = SIDE_Y // PIECES
+    got = (got_up, got_down)
+    going = {}
+
+    def target_of(way, step):
+        offset = step_counts[way] - step
+        return wrap(z_at + (1 - 2 * way) * offset, side_z)
+
+    def start(way, step, piece):
+        rows = pl.ds(piece * span, span)
+        if step == 0:
+            block = part_ref.at[rows, target_of(way, 0)]
+        else:
+            block = got[way].at[step - 1, rows]
+        at = (way, step, piece)
+        going[at] = send(
+            block,
+            got[way].at[step, rows],
+            (z_send.at[at], z_recv.at[at]),
+            along_z(1 - 2 * way),
+        )
+
+    for piece in range(PIECES):
+        for way in range(2):
+            start(way, 0, piece)
+    for step in range(step_counts[0] - 1):
+        for piece in range(PIECES):
+            for way in range(2):
+                if step + 1 < step_counts[way]:
+                    going[(way, step, piece)].wait_recv()
+                    place = target_of(way, step + 1)
+
+                    def add_own(row, carry, way=way, step=step, place=place):
+                        held = got[way][step, row].astype(jnp.float32)
+                        mine = part_ref[row, place].astype(jnp.float32)
+                        got[way][step, row] = (held + mine).astype(jnp.bfloat16)
+                        return carry
+
+                    lax.fori_loop(piece * span, (piece + 1) * span, add_own, 0)
+                    start(way, step + 1, piece)
+    for way in range(2):
+        for piece in range(PIECES):
+            going[(way, step_counts[way] - 1, piece)].wait_recv()
+
+    def close(row, carry):
+        total = part_ref[row, z_at].astype(jnp.float32)
+        total = total + got_up[step_counts[0] - 1, row].astype(jnp.float32)
+        total = total + got_down[step_counts[1] - 1, row].astype(jnp.float32)
+        y_held[row] = total.astype(jnp.bfloat16)
+        return carry
+
+    lax.fori_loop(0, SIDE_Y, close, 0)
+    far = send(
+        y_held.at[wrap(y_at + 2, SIDE_Y)], y_got.at[0], (y_send.at[0], y_recv.at[0]), along_y(1)
+    )
+    down = send(
+        y_held.at[wrap(y_at - 1, SIDE_Y)], y_got.at[1], (y_send.at[1], y_recv.at[1]), along_y(-1)
+    )
+    far.wait_recv()
+    up_row = y_held[wrap(y_at + 1, SIDE_Y)].astype(jnp.float32)
+    y_got[0] = (y_got[0].astype(jnp.float32) + up_row).astype(jnp.bfloat16)
+    near = send(y_got.at[0], y_got.at[2], (y_send.at[2], y_recv.at[2]), along_y(1))
+    down.wait_recv()
+    near.wait_recv()
+    total = y_held[y_at].astype(jnp.float32) + y_got[1].astype(jnp.float32)
+    sum_ref[...] = (total + y_got[2].astype(jnp.float32)).astype(jnp.bfloat16)
+    for copy in [far, down, near] + list(going.values()):
+        copy.wait_send()
+
+
+def scatter_sums(parts, side_z):
+    all_rows, columns = parts.shape
+    rows = all_rows // (SIDE_Y * side_z)
+    up_steps, down_steps = steps_of(side_z)
+    return pl.pallas_call(
+        functools.partial(scatter_kernel, side_z),
+        out_shape=jax.ShapeDtypeStruct((rows, columns), parts.dtype),
+        in_specs=[pl.BlockSpec(memory_space=pltpu.VMEM)],
+        out_specs=pl.BlockSpec(memory_space=pltpu.VMEM),
+        scratch_shapes=[
+            pltpu.VMEM((up_steps, SIDE_Y, rows, columns), parts.dtype),
+            pltpu.VMEM((down_steps, SIDE_Y, rows, columns), parts.dtype),
+            pltpu.VMEM((SIDE_Y, rows, columns), parts.dtype),
+            pltpu.VMEM((3, rows, columns), parts.dtype),
+            pltpu.SemaphoreType.DMA((2, up_steps, PIECES)),
+            pltpu.SemaphoreType.DMA((2, up_steps, PIECES)),
+            pltpu.SemaphoreType.DMA((3,)),
+            pltpu.SemaphoreType.DMA((3,)),
+        ],
+        compiler_params=pltpu.CompilerParams(
+            collective_id=1, has_side_effects=True, vmem_limit_bytes=32 * 2**20
+        ),
+        cost_estimate=pl.CostEstimate(
+            flops=0, bytes_accessed=200 * 2**20, transcendentals=0
+        ),
+    )(parts.reshape(SIDE_Y, side_z, rows, columns))
 
 
 def shards(tokens, cotangent, routes, mix_weights, w_gate, w_up, w_down):
@@ -49,9 +273,7 @@
         [my_routes.astype(jnp.bfloat16), *split_three(my_mix)], axis=1
     )
     extra = jnp.pad(extra, ((0, 0), (0, 128 - extra.shape[1])))
-    rows = lax.all_gather(
-        jnp.concatenate([both, extra], axis=1), "expert", axis=0, tiled=True
-    )
+    rows = gather_rows(jnp.concatenate([both, extra], axis=1), owner_count // SIDE_Y)
     x_rows = rows[:, :width]
     c_rows = rows[:, width : 2 * width]
     tail = rows[:, 2 * width : 2 * width + 4 * picks_per].astype(jnp.float32)
@@ -73,17 +295,14 @@
 
     mixed_part = contract(hidden_mix, w_out, 1, 1).astype(jnp.bfloat16)
     grad_part = contract(in_back, w_in, 1, 1).astype(jnp.bfloat16)
-    sums = lax.psum_scatter(
-        jnp.concatenate([mixed_part, grad_part], axis=1),
-        "expert",
-        scatter_dimension=0,
-        tiled=True,
-    )
     in_grad = contract(x_rows, in_back, 0, 0).astype(jnp.bfloat16)
     out_grad = contract(c_rows, hidden_mix, 0, 0).astype(jnp.bfloat16)
     weight_grads = lax.psum_scatter(
         jnp.concatenate([in_grad, out_grad], axis=1), "dp", scatter_dimension=0, tiled=True
     ).astype(jnp.float32)
+    sums = scatter_sums(
+        jnp.concatenate([mixed_part, grad_part], axis=1), owner_count // SIDE_Y
+    )
     sums = sums.reshape(sub_rows, 2, dp_count, width_dev).transpose(1, 2, 0, 3)
     sums = lax.all_to_all(sums, "dp", split_axis=1, concat_axis=1, tiled=True)
     sums = sums.reshape(2, tok_rows, width_dev)

time: 1040 us -> 308 us (0.30)
  waiting for transfers between devices: 942 us -> 4.91 us
  Pallas kernels: 0 us -> 208 us
  starting transfers between devices: 25.4 us -> 10.2 us
  blocking collectives: 0 us -> 13.2 us
    reduce_scatter x1 -> x0, waiting for transfers between devices: 718 us -> none  [shards(): lax.psum_scatter(jnp.concatenate([mixed_part, grad_part], axis=1), 'exper...]
    pallas_call x0 -> x2, Pallas kernels: none -> 208 us  [the longest x1 108 us: gather_rows(): pl.pallas_call(functools.partial(gather_kernel, side_z), out_shape=jax.Sh...]
    all_gather x1 -> x0, waiting for transfers between devices: 144 us -> none  [shards(): lax.all_gather(jnp.concatenate([both, extra], axis=1), 'expert', axis=0,...]
    all_gather x1, waiting for transfers between devices: 49 us -> 0.02 us  [shards(): weights = lax.all_gather(weights_dev, 'dp', axis=0, tiled=True)]
    reduce_scatter x1, waiting for transfers between devices: 24.4 us -> 0.01 us  [shards(): lax.psum_scatter(jnp.concatenate([in_grad, out_grad], axis=1), 'dp', scat...]
    all_to_all x1 -> x0, starting transfers between devices: 15 us -> none  [shards(): sums = lax.all_to_all(sums, 'dp', split_axis=1, concat_axis=1, tiled=True)]
    all_to_all x0 -> x1, blocking collectives: none -> 13.2 us  [shards(): sums = lax.all_to_all(sums, 'dp', split_axis=1, concat_axis=1, tiled=True)]
  transfers between devices with their start and end apart: 6 -> 3, of which waited for: 6 -> 1; matrix products, arithmetic and copies ran while one was open for 3% -> 8% of each run, Pallas kernels for 0% -> 68%
where the time goes in v2:
time: 308 us
  Pallas kernels  208 us (68%)
  matrix products  27.9 us (9%)
  other arithmetic  14.8 us (5%)
  local copies, waits for them, and re-layouts  14.7 us (5%)
  between operations  14.3 us (5%)
  blocking collectives  13.2 us (4%)
  starting transfers between devices  10.2 us (3%)
  waiting for transfers between devices  4.91 us (2%)
    pallas_call x1, Pallas kernels, gather_rows(): pl.pallas_call(functools.partial(gather_kernel, side_z), out_shape=jax.Sh...  108 us
    pallas_call x1, Pallas kernels, scatter_sums(): pl.pallas_call(functools.partial(scatter_kernel, side_z), out_shape=jax.S...  100 us
    dot_general x6, matrix products, contract(): lax.dot_general(left_side, right_side, (((left_dim,), (right_dim,)), ((),...  27.9 us
    all_to_all x1, blocking collectives, shards(): sums = lax.all_to_all(sums, 'dp', split_axis=1, concat_axis=1, tiled=True)  13.2 us
    unnamed x29, local copies, waits for them, and re-layouts  12.5 us
    all_to_all x1, starting transfers between devices, shards(): both = lax.all_to_all(both, 'dp', split_axis=1, concat_axis=1, tiled=True)  10.1 us
    concatenate x1, other arithmetic, shards(): jnp.concatenate([mixed_part, grad_part], axis=1)  8.25 us
  transfers between devices with their start and end apart: 3, of which 1 were waited for; matrix products, arithmetic and copies ran while one was open for 8% of the time, Pallas kernels for 68%

profile of v2, /device:TPU:1, one launch (start us, length us, event | category | flops | bytes accessed | tf_op | source)
XLA Modules:
  0.0 307.9 jit_solution(1148198263591694698)
XLA Ops:
  7.2 1.1 copy.58
  8.3 1.1 copy.59
  9.4 1.8 pad_maximum_fusion.5
  11.2 0.9 pad_maximum_fusion.7
  12.1 0.8 copy.54
  12.9 10.1 %all-to-all-start = ((bf16[2,8,16,256]{3,0,2,1:T(2,128)(2,1)}), bf16[2,8,16,256]{3,0,2,1:T(2,128)(2,1)S(1)}, u32[]{:S(2)}, u32[]{:S(2)}) async-start(bf16[2,8,16,256]{3,0,2,1:T(2,128)(2,1)} %copy.54), calls=%async_computation | async-start | bytes 262144 | tf_op jit(solution)/shard_map/all_to_all | solution.py:268
  23.0 0.1 constant_dynamic-slice_fusion
  23.4 0.1 fusion.31
  23.4 4.9 %all-to-all-done = bf16[2,8,16,256]{3,0,2,1:T(2,128)(2,1)S(1)} async-done(((bf16[2,8,16,256]{3,0,2,1:T(2,128)(2,1)}), bf16[2,8,16,256]{3,0,2,1:T(2,128)(2,1)S(1)}, u32[]{:S(2)}, u32[]{:S(2)}) %all-to-all-start) | async-done | bytes 131104 | tf_op jit(solution)/shard_map/all_to_all | solution.py:268
  28.3 0.1 copy.55
  28.4 107.8 %shard_map.110 = bf16[4,16,16,4224]{3,2,1,0:T(8,128)(2,1)S(1)} custom-call(bf16[16,4224]{1,0:T(8,128)(2,1)S(1)} %pad_maximum_fusion.6.own_ref), custom_call_target="tpu_custom_call" | custom-call | bytes 209715200 | tf_op jit(solution)/shard_map/pallas_call | solution.py:124
  136.3 3.3 %copy-done.2 = bf16[4,16,16,4224]{3,2,1,0:T(8,128)(2,1)} copy-done((bf16[4,16,16,4224]{3,2,1,0:T(8,128)(2,1)}, bf16[4,16,16,4224]{3,2,1,0:T(8,128)(2,1)S(1)}, u32[]{:S(2)}) %copy-start.2) | copy-done | bytes 8650776
  139.7 0.1 copy.68
  139.9 6.3 %fusion.6 = f32[1024,768]{0,1:T(8,128)S(1)} fusion(bf16[1024,4224]{1,0:T(8,128)(2,1)} %bitcast.36, bf16[2048,1152]{0,1:T(8,128)(2,1)} %all-gather.2.cloned.1.call-done), kind=kOutput, calls=%fused_computation.10 | convolution fusion | flops 3221225472 | bytes 10485760 | tf_op jit(solution)/shard_map/dot_general | solution.py:12
  146.2 5.1 %multiply_convert_fusion.1 = (bf16[1024,384]{0,1:T(8,128)(2,1)S(1)}, bf16[1024,384]{0,1:T(8,128)(2,1)S(1)}, bf16[1024,384]{0,1:T(8,128)(2,1)S(1)}) fusion(f32[1024,768]{0,1:T(8,128)S(1)} %fusion.6, f32[1024]{0:T(1024)S(1)} %fusion.23, bf16[2048,1152]{0,1:T(8,128)(2,1)} %all-gather.2.cloned.1.call-done, bf16[1024,4224]{1,0:T(8,128)(2,1)} %bitcast.37), kind=kOutput, calls=%fused_computation.18 | convolution fusion | flops 1617297408 | bytes 11276288 | tf_op jit(solution)/shard_map/dot_general | solution.py:12
  151.4 1.8 fusion.11
  153.2 3.6 %fusion.8 = bf16[2048,768]{0,1:T(8,128)(2,1)S(1)} fusion(bf16[1024,4224]{1,0:T(8,128)(2,1)S(1)} %bitcast.41, bf16[1024,384]{0,1:T(8,128)(2,1)S(1)} %get-tuple-element.31, bf16[1024,384]{0,1:T(8,128)(2,1)S(1)} %get-tuple-element.30), kind=kOutput, calls=%fused_computation.12 | convolution fusion | flops 3225944064 | bytes 8912896 | tf_op jit(solution)/shard_map/dot_general | solution.py:12
  156.8 2.6 pad_maximum_fusion.1
  159.4 6.0 %convolution_convert_fusion = bf16[1024,2048]{1,0:T(8,128)(2,1)} fusion(bf16[1024,384]{0,1:T(8,128)(2,1)S(1)} %get-tuple-element.32, bf16[2048,1152]{0,1:T(8,128)(2,1)} %all-gather.2.cloned.1.call-done), kind=kOutput, calls=%fused_computation.2 | convolution fusion | flops 1612709888 | bytes 6553600 | tf_op jit(solution)/shard_map/dot_general | solution.py:12
  165.4 5.1 %convolution_convert_fusion.1 = bf16[1024,2048]{1,0:T(8,128)(2,1)} fusion(bf16[2048,1152]{0,1:T(8,128)(2,1)S(1)} %bitcast.56, bf16[1024,384]{0,1:T(8,128)(2,1)S(1)} %get-tuple-element.31, bf16[1024,384]{0,1:T(8,128)(2,1)S(1)} %get-tuple-element.30), kind=kOutput, calls=%fused_computation.3 | convolution fusion | flops 3226468352 | bytes 8912896 | tf_op jit(solution)/shard_map/dot_general | solution.py:12
  170.5 8.2 %pad_maximum_fusion = bf16[1024,4096]{1,0:T(8,128)(2,1)} fusion(bf16[1024,2048]{1,0:T(8,128)(2,1)} %convolution_convert_fusion.1, bf16[1024,2048]{1,0:T(8,128)(2,1)} %convolution_convert_fusion), kind=kLoop, calls=%fused_computation | loop fusion | flops 16777216 | bytes 16777216 | tf_op jit(solution)/shard_map/concatenate | solution.py:304
  178.8 3.6 %copy-done.1 = bf16[1024,4096]{1,0:T(8,128)(2,1)S(1)} copy-done((bf16[1024,4096]{1,0:T(8,128)(2,1)S(1)}, bf16[1024,4096]{1,0:T(8,128)(2,1)}, u32[]{:S(2)}) %copy-start.1) | copy-done | bytes 8388632
  182.3 100.1 %shard_map.111 = bf16[16,4096]{1,0:T(8,128)(2,1)S(1)} custom-call(bf16[4,16,16,4096]{3,2,1,0:T(8,128)(2,1)S(1)} %bitcast.34), custom_call_target="tpu_custom_call" | custom-call | bytes 209715200 | tf_op jit(solution)/shard_map/pallas_call | solution.py:229
  282.5 0.1 copy.74
  282.6 13.2 %all_to_all.10 = bf16[2,8,16,256]{3,0,2,1:T(2,128)(2,1)S(1)} all-to-all(bf16[2,8,16,256]{3,0,2,1:T(2,128)(2,1)S(1)} %bitcast.49), channel_id=1, replica_groups=mesh['dp'=8,'expert'=64] {'dp'}, dimensions={1} | all-to-all | bytes 262144 | tf_op jit(solution)/shard_map/all_to_all | solution.py:307
  295.8 0.2 fusion.34
  296.0 0.6 copy.70
  296.6 0.6 copy.69
  297.3 1.1 convert_element_type.62
  298.4 0.8 slice_bitcast_fusion
  299.3 0.9 copy.65
  300.2 0.9 copy.64
  (35 shorter events, 0.5 us)
Async XLA Ops:
  7.2 15.9 %copy-start = (f32[128,8]{0,1:T(8,128)S(1)}, f32[128,8]{0,1:T(8,128)}, u32[]{:S(2)}) copy-start(f32[128,8]{0,1:T(8,128)} %param.10) | copy-start | bytes 12292
  7.2 16.0 %copy-start.3 = (s32[128,8]{0,1:T(8,128)S(1)}, s32[128,8]{0,1:T(8,128)}, u32[]{:S(2)}) copy-start(s32[128,8]{0,1:T(8,128)} %param.9) | copy-start | bytes 12292
  7.2 132.7 %all-gather.2.cloned.1.call-start = ((), (), s32[]{:S(2)}) async-start(), calls=%async_computation.3 | async-start | bytes 5308416 | tf_op jit(solution)/shard_map/all_gather | solution.py:265
  12.9 15.4 %all-to-all-start = ((bf16[2,8,16,256]{3,0,2,1:T(2,128)(2,1)}), bf16[2,8,16,256]{3,0,2,1:T(2,128)(2,1)S(1)}, u32[]{:S(2)}, u32[]{:S(2)}) async-start(bf16[2,8,16,256]{3,0,2,1:T(2,128)(2,1)} %copy.54), calls=%async_computation | async-start | bytes 262144 | tf_op jit(solution)/shard_map/all_to_all | solution.py:268
  23.0 274.3 %reduce-scatter.2.cloned.1.call-start = ((), (), s32[]{:S(2)}) async-start(), calls=%async_computation.4 | async-start | bytes 5308416 | tf_op jit(solution)/shard_map/reduce_scatter | solution.py:300
  136.3 3.4 %copy-start.2 = (bf16[4,16,16,4224]{3,2,1,0:T(8,128)(2,1)}, bf16[4,16,16,4224]{3,2,1,0:T(8,128)(2,1)S(1)}, u32[]{:S(2)}) copy-start(bf16[4,16,16,4224]{3,2,1,0:T(8,128)(2,1)S(1)} %shard_map.110) | copy-start | bytes 25952260
  139.9 11.5 %slice-start = ((s8[8650752]{0:T(1024)(128)(4,1)}), s8[4194304]{0:T(1024)(128)(4,1)S(1)}, s32[]{:S(2)}) async-start(s8[8650752]{0:T(1024)(128)(4,1)} %bitcast.38), calls=%async_computation.5 | async-start | bytes 8388608
  139.9 11.5 %slice-start.1 = ((s8[8650752]{0:T(1024)(128)(4,1)}), s8[4194304]{0:T(1024)(128)(4,1)S(1)}, s32[]{:S(2)}) async-start(s8[8650752]{0:T(1024)(128)(4,1)} %bitcast.38), calls=%async_computation.6 | async-start | bytes 8388608
  146.2 5.1 %slice-start.2 = ((s8[8650752]{0:T(1024)(128)(4,1)}), s8[262144]{0:T(1024)(128)(4,1)S(1)}, s32[]{:S(2)}) async-start(s8[8650752]{0:T(1024)(128)(4,1)} %bitcast.38), calls=%async_computation.7 | async-start | bytes 524288
  159.4 6.0 %slice-start.3 = ((s8[4718592]{0:T(1024)(128)(4,1)}), s8[524288]{0:T(1024)(128)(4,1)S(1)}, s32[]{:S(2)}) async-start(s8[4718592]{0:T(1024)(128)(4,1)} %bitcast.55), calls=%async_computation.8 | async-start | bytes 1048576
  159.4 6.0 %slice-start.4 = ((s8[4718592]{0:T(1024)(128)(4,1)}), s8[4194304]{0:T(1024)(128)(4,1)S(1)}, s32[]{:S(2)}) async-start(s8[4718592]{0:T(1024)(128)(4,1)} %bitcast.55), calls=%async_computation.9 | async-start | bytes 8388608
  178.8 3.6 %copy-start.1 = (bf16[1024,4096]{1,0:T(8,128)(2,1)S(1)}, bf16[1024,4096]{1,0:T(8,128)(2,1)}, u32[]{:S(2)}) copy-start(bf16[1024,4096]{1,0:T(8,128)(2,1)} %pad_maximum_fusion) | copy-start | bytes 25165828
Sparse Core Ops, SparseCore 0:
  11.4 51.0 all-gather.1
  159.5 40.2 reduce-scatter.1

commit v3 on v2

v3 whole, which is shorter than its diff:
```python
import functools

import jax
import jax.numpy as jnp
from jax import lax
from jax.experimental import pallas as pl
from jax.experimental.pallas import tpu as pltpu
from jax.sharding import PartitionSpec as P


def contract(left_side, right_side, left_dim, right_dim):
    return lax.dot_general(
        left_side,
        right_side,
        (((left_dim,), (right_dim,)), ((), ())),
        preferred_element_type=jnp.float32,
    )


def silu_parts(gate_in):
    logistic = jax.nn.sigmoid(gate_in)
    return (gate_in * logistic, logistic * (1.0 + gate_in * (1.0 - logistic)))


def split_three(values):
    high = values.astype(jnp.bfloat16)
    rest = values - high.astype(jnp.float32)
    middle = rest.astype(jnp.bfloat16)
    low = (rest - middle.astype(jnp.float32)).astype(jnp.bfloat16)
    return (high, middle, low)


SIDE_Y = 4
PIECES = 2


def steps_of(count):
    return (count // 2, count - 1 - count // 2)


def ring_places(side_z):
    me = lax.axis_index("expert")
    y_at, z_at = me // side_z, lax.rem(me, side_z)

    def along_z(offset):
        return {"expert": y_at * side_z + lax.rem(z_at + offset + side_z, side_z)}

    def along_y(offset):
        return {"expert": lax.rem(y_at + offset + SIDE_Y, SIDE_Y) * side_z + z_at}

    return (y_at, z_at, along_y, along_z)


def greet(places):
    barrier = pltpu.get_barrier_semaphore()
    for place in places:
        pl.semaphore_signal(
            barrier, inc=1, device_id=place, device_id_type=pl.DeviceIdType.MESH
        )
    pl.semaphore_wait(barrier, len(places))


def send(source, target, sems, place):
    copy = pltpu.make_async_remote_copy(
        src_ref=source,
        dst_ref=target,
        send_sem=sems[0],
        recv_sem=sems[1],
        device_id=place,
        device_id_type=pl.DeviceIdType.MESH,
    )
    copy.start()
    return copy


def wrap(value, count):
    return lax.rem(value + 2 * count, count)


def gather_kernel(side_z, x_own, c_own, x_all, c_all, xz_send, xz_recv, xy_send, xy_recv,
                  cy_send, cy_recv, cz_send, cz_recv, own_sem):
    y_at, z_at, along_y, along_z = ring_places(side_z)
    own_copies = [
        pltpu.make_async_copy(x_own, x_all.at[y_at, z_at], own_sem.at[0]),
        pltpu.make_async_copy(c_own, c_all.at[y_at, z_at], own_sem.at[1]),
    ]
    for copy in own_copies:
        copy.start()
    greet([along_y(1), along_y(-1), along_z(1), along_z(-1)])
    for copy in own_copies:
        copy.wait()
    step_counts = steps_of(side_z)
    span = SIDE_Y // PIECES
    up_y, down_y = wrap(y_at - 1, SIDE_Y), wrap(y_at + 1, SIDE_Y)
    xz, xy, cz = {}, {}, {}

    def start_xz(way, step):
        sign = 1 - 2 * way
        block = x_all.at[y_at, wrap(z_at - sign * step, side_z)]
        at = (way, step)
        xz[at] = send(block, block, (xz_send.at[at], xz_recv.at[at]), along_z(sign))

    def place_of(number):
        sign = 1 if number % 2 else -1
        return wrap(z_at - sign * ((number + 1) // 2), side_z)

    def start_xy(number, hop):
        row = up_y if hop == 2 else y_at
        block = x_all.at[row, place_of(number)]
        at = (number, hop)
        xy[at] = send(
            block, block, (xy_send.at[at], xy_recv.at[at]), along_y(-1 if hop == 1 else 1)
        )

    def start_cz(way, step, piece):
        sign = 1 - 2 * way
        block = c_all.at[pl.ds(piece * span, span), wrap(z_at - sign * step, side_z)]
        at = (way, step, piece)
        cz[at] = send(block, block, (cz_send.at[at], cz_recv.at[at]), along_z(sign))

    start_xz(0, 0)
    start_xz(1, 0)
    mine = c_all.at[y_at, z_at]
    first = send(mine, mine, (cy_send.at[0], cy_recv.at[0]), along_y(1))
    other = send(mine, mine, (cy_send.at[1], cy_recv.at[1]), along_y(-1))
    start_xy(0, 0)
    start_xy(0, 1)
    first.wait_recv()
    below = c_all.at[up_y, z_at]
    second = send(below, below, (cy_send.at[2], cy_recv.at[2]), along_y(1))
    other.wait_recv()
    second.wait_recv()
    for piece in range(PIECES):
        for way in range(2):
            start_cz(way, 0, piece)
    passed = 0
    arrived = 1
    for step in range(step_counts[0]):
        ready = arrived
        for way in range(2):
            if step < step_counts[way]:
                xz[(way, step)].wait_recv()
                if step + 1 < step_counts[way]:
                    start_xz(way, step + 1)
                start_xy(2 * step + 1 + way, 0)
                start_xy(2 * step + 1 + way, 1)
                arrived += 1
        for number in range(passed, ready):
            xy[(number, 0)].wait_recv()
            start_xy(number, 2)
        passed = ready
        for piece in range(PIECES):
            for way in range(2):
                if step < step_counts[way]:
                    cz[(way, step, piece)].wait_recv()
                    if step + 1 < step_counts[way]:
                        start_cz(way, step + 1, piece)
    for number in range(passed, side_z):
        xy[(number, 0)].wait_recv()
        start_xy(number, 2)
    for number in range(side_z):
        xy[(number, 1)].wait_recv()
        xy[(number, 2)].wait_recv()
    for group in (xz, xy, cz):
        for copy in group.values():
            copy.wait_send()
    for copy in (first, other, second):
        copy.wait_send()


def gather_rows(x_own, c_own, side_z):
    rows = x_own.shape[0]
    longest = steps_of(side_z)[0]
    vmem = pl.BlockSpec(memory_space=pltpu.VMEM)
    sem = pltpu.SemaphoreType.DMA
    gathered = pl.pallas_call(
        functools.partial(gather_kernel, side_z),
        out_shape=[
            jax.ShapeDtypeStruct((SIDE_Y, side_z, *own.shape), own.dtype)
            for own in (x_own, c_own)
        ],
        in_specs=[vmem, vmem],
        out_specs=[vmem, vmem],
        scratch_shapes=[
            sem((2, longest)),
            sem((2, longest)),
            sem((side_z, 3)),
            sem((side_z, 3)),
            sem((3,)),
            sem((3,)),
            sem((2, longest, PIECES)),
            sem((2, longest, PIECES)),
            sem((2,)),
        ],
        compiler_params=pltpu.CompilerParams(
            collective_id=0, has_side_effects=True, vmem_limit_bytes=24 * 2**20
        ),
        cost_estimate=pl.CostEstimate(
            flops=0, bytes_accessed=200 * 2**20, transcendentals=0
        ),
    )(x_own, c_own)
    return [whole.reshape(SIDE_Y * side_z * rows, -1) for whole in gathered]


def scatter_kernel(side_z, m_part, g_part, m_sum, g_sum, m_up, m_down, m_held, m_got,
                   g_y, g_held, g_up, g_down, mz_send, mz_recv, my_send, my_recv,
                   gy_send, gy_recv, gz_send, gz_recv):
    y_at, z_at, along_y, along_z = ring_places(side_z)
    greet([along_y(1), along_y(-1), along_z(1), along_z(-1)])
    step_counts = steps_of(side_z)
    span = SIDE_Y // PIECES
    half = side_z // 2
    m_slots, g_slots = (m_up, m_down), (g_up, g_down)
    mz, gz, gy = {}, {}, {}

    def rounded_sum(*terms):
        total = terms[0].astype(jnp.float32)
        for term in terms[1:]:
            total = total + term.astype(jnp.float32)
        return total.astype(jnp.bfloat16)

    def target_of(way, step):
        return wrap(z_at + (1 - 2 * way) * (step_counts[way] - step), side_z)

    def start_mz(way, step, piece):
        rows = pl.ds(piece * span, span)
        block = m_part.at[rows, target_of(way, 0)] if step == 0 else m_slots[way].at[step - 1, rows]
        at = (way, step, piece)
        mz[at] = send(
            block, m_slots[way].at[step, rows], (mz_send.at[at], mz_recv.at[at]), along_z(1 - 2 * way)
        )

    def start_gz(way, step):
        block = g_held.at[target_of(way, 0)] if step == 0 else g_slots[way].at[step - 1]
        at = (way, step)
        gz[at] = send(
            block, g_slots[way].at[step], (gz_send.at[at], gz_recv.at[at]), along_z(1 - 2 * way)
        )

    def start_gy(slot, source, way):
        gy[slot] = send(
            source, g_y.at[slot], (gy_send.at[slot], gy_recv.at[slot]), along_y(1 - 2 * way)
        )

    low, high = pl.ds(0, half), pl.ds(half, half)
    above, below, across = wrap(y_at + 1, SIDE_Y), wrap(y_at - 1, SIDE_Y), wrap(y_at + 2, SIDE_Y)

    def pass_far():
        for slot, row, first, way in ((0, above, 0, 0), (1, below, half, 1)):
            gy[slot].wait_recv()

            def add_row(place, carry, slot=slot, row=row, first=first):
                g_y[slot, place] = rounded_sum(g_y[slot, place], g_part[row, first + place])
                return carry

            lax.fori_loop(0, half, add_row, 0)
            start_gy(4 + slot, g_y.at[slot], way)

    def close_y():
        for slot in (2, 3, 4, 5):
            gy[slot].wait_recv()

        def add_low(place, carry):
            g_held[place] = rounded_sum(g_part[y_at, place], g_y[4, place], g_y[3, place])
            return carry

        def add_high(place, carry):
            g_held[half + place] = rounded_sum(
                g_part[y_at, half + place], g_y[2, place], g_y[5, place]
            )
            return carry

        lax.fori_loop(0, half, add_low, 0)
        lax.fori_loop(0, half, add_high, 0)
        start_gz(0, 0)
        start_gz(1, 0)

    def step_gz(step):
        for way in range(2):
            if step + 1 < step_counts[way]:
                gz[(way, step)].wait_recv()
                slot = g_slots[way]
                slot[step] = rounded_sum(slot[step], g_held[target_of(way, step + 1)])
                start_gz(way, step + 1)

    for piece in range(PIECES):
        for way in range(2):
            start_mz(way, 0, piece)
    start_gy(0, g_part.at[across, low], 0)
    start_gy(1, g_part.at[across, high], 1)
    start_gy(2, g_part.at[above, high], 0)
    start_gy(3, g_part.at[below, low], 1)
    middle = step_counts[0] // 2
    g_step = 0
    for step in range(step_counts[0] - 1):
        for piece in range(PIECES):
            for way in range(2):
                if step + 1 < step_counts[way]:
                    mz[(way, step, piece)].wait_recv()
                    place = target_of(way, step + 1)

                    def add_own(row, carry, way=way, step=step, place=place):
                        slot = m_slots[way]
                        slot[step, row] = rounded_sum(slot[step, row], m_part[row, place])
                        return carry

                    lax.fori_loop(piece * span, (piece + 1) * span, add_own, 0)
                    start_mz(way, step + 1, piece)
            if step > middle:
                step_gz(g_step)
                g_step += 1
        if step == 1:
            pass_far()
        if step == middle:
            close_y()
    for way in range(2):
        for piece in range(PIECES):
            mz[(way, step_counts[way] - 1, piece)].wait_recv()

    def close_z(row, carry):
        m_held[row] = rounded_sum(
            m_part[row, z_at], m_up[step_counts[0] - 1, row], m_down[step_counts[1] - 1, row]
        )
        return carry

    lax.fori_loop(0, SIDE_Y, close_z, 0)
    far = send(m_held.at[across], m_got.at[0], (my_send.at[0], my_recv.at[0]), along_y(1))
    down = send(m_held.at[below], m_got.at[1], (my_send.at[1], my_recv.at[1]), along_y(-1))
    if g_step < step_counts[0] - 1:
        step_gz(g_step)
        g_step += 1
    far.wait_recv()
    m_got[0] = rounded_sum(m_got[0], m_held[above])
    near = send(m_got.at[0], m_got.at[2], (my_send.at[2], my_recv.at[2]), along_y(1))
    while g_step < step_counts[0] - 1:
        step_gz(g_step)
        g_step += 1
    down.wait_recv()
    near.wait_recv()
    m_sum[...] = rounded_sum(m_held[y_at], m_got[1], m_got[2])
    for way in range(2):
        gz[(way, step_counts[way] - 1)].wait_recv()
    g_sum[...] = rounded_sum(
        g_held[z_at], g_up[step_counts[0] - 1], g_down[step_counts[1] - 1]
    )
    for group in (mz, gz, gy):
        for copy in group.values():
            copy.wait_send()
    for copy in (far, down, near):
        copy.wait_send()


def scatter_sums(m_part, g_part, side_z):
    all_rows, columns = m_part.shape
    rows = all_rows // (SIDE_Y * side_z)
    up_steps, down_steps = steps_of(side_z)
    kind = m_part.dtype
    vmem = pl.BlockSpec(memory_space=pltpu.VMEM)
    sem = pltpu.SemaphoreType.DMA
    whole = (SIDE_Y, side_z, rows, columns)
    return pl.pallas_call(
        functools.partial(scatter_kernel, side_z),
        out_shape=[jax.ShapeDtypeStruct((rows, columns), kind)] * 2,
        in_specs=[vmem, vmem],
        out_specs=[vmem, vmem],
        scratch_shapes=[
            pltpu.VMEM((up_steps, SIDE_Y, rows, columns), kind),
            pltpu.VMEM((down_steps, SIDE_Y, rows, columns), kind),
            pltpu.VMEM((SIDE_Y, rows, columns), kind),
            pltpu.VMEM((3, rows, columns), kind),
            pltpu.VMEM((6, side_z // 2, rows, columns), kind),
            pltpu.VMEM((side_z, rows, columns), kind),
            pltpu.VMEM((up_steps, rows, columns), kind),
            pltpu.VMEM((down_steps, rows, columns), kind),
            sem((2, up_steps, PIECES)),
            sem((2, up_steps, PIECES)),
            sem((3,)),
            sem((3,)),
            sem((6,)),
            sem((6,)),
            sem((2, up_steps)),
            sem((2, up_steps)),
        ],
        compiler_params=pltpu.CompilerParams(
            collective_id=1, has_side_effects=True, vmem_limit_bytes=32 * 2**20
        ),
        cost_estimate=pl.CostEstimate(
            flops=0, bytes_accessed=200 * 2**20, transcendentals=0
        ),
    )(m_part.reshape(whole), g_part.reshape(whole))


def shards(tokens, cotangent, routes, mix_weights, w_gate, w_up, w_down):
    tok_rows, width_dev = tokens.shape
    picks_per = routes.shape[1]
    dp_count = lax.axis_size("dp")
    owner_count = lax.axis_size("expert")
    hidden = w_gate.shape[2]
    sub_rows = tok_rows // dp_count
    width = width_dev * dp_count
    me_dp = lax.axis_index("dp")
    me_expert = lax.axis_index("expert")

    weights_dev = jnp.concatenate([w_gate[0], w_up[0], w_down[0].T], axis=1)
    weights = lax.all_gather(weights_dev, "dp", axis=0, tiled=True)

    both = jnp.stack([tokens, cotangent]).reshape(2, dp_count, sub_rows, width_dev)
    both = lax.all_to_all(both, "dp", split_axis=1, concat_axis=1, tiled=True)
    both = both.transpose(0, 2, 1, 3).reshape(2, sub_rows, width)
    my_routes = lax.dynamic_slice_in_dim(routes, me_dp * sub_rows, sub_rows, 0)
    my_mix = lax.dynamic_slice_in_dim(mix_weights, me_dp * sub_rows, sub_rows, 0)
    extra = jnp.concatenate(
        [my_routes.astype(jnp.bfloat16), *split_three(my_mix)], axis=1
    )
    extra = jnp.pad(extra, ((0, 0), (0, 128 - extra.shape[1])))
    x_rows, c_wide = gather_rows(
        both[0], jnp.concatenate([both[1], extra], axis=1), owner_count // SIDE_Y
    )
    c_rows = c_wide[:, :width]
    tail = c_wide[:, width : width + 4 * picks_per].astype(jnp.float32)
    tail = tail.reshape(-1, 4, picks_per)
    mix_all = tail[:, 1] + tail[:, 2] + tail[:, 3]
    named = tail[:, 0] == me_expert.astype(jnp.float32)
    weight_row = jnp.sum(jnp.where(named, mix_all, 0.0), axis=1, keepdims=True)

    w_in = weights[:, : 2 * hidden]
    w_out = weights[:, 2 * hidden :]
    pre = contract(x_rows, w_in, 1, 0)
    back_hidden = contract(c_rows, w_out, 1, 0) * weight_row
    gate_in, up_in = pre[:, :hidden], pre[:, hidden:]
    activated, slope_silu = silu_parts(gate_in)
    hidden_mix = (activated * up_in * weight_row).astype(jnp.bfloat16)
    gate_back = (back_hidden * up_in * slope_silu).astype(jnp.bfloat16)
    up_back = (back_hidden * activated).astype(jnp.bfloat16)
    in_back = jnp.concatenate([gate_back, up_back], axis=1)

    mixed_part = contract(hidden_mix, w_out, 1, 1).astype(jnp.bfloat16)
    grad_part = contract(in_back, w_in, 1, 1).astype(jnp.bfloat16)
    in_grad = contract(x_rows, in_back, 0, 0).astype(jnp.bfloat16)
    out_grad = contract(c_rows, hidden_mix, 0, 0).astype(jnp.bfloat16)
    weight_grads = lax.psum_scatter(
        jnp.concatenate([in_grad, out_grad], axis=1), "dp", scatter_dimension=0, tiled=True
    ).astype(jnp.float32)
    sums = jnp.stack(scatter_sums(mixed_part, grad_part, owner_count // SIDE_Y))
    sums = sums.reshape(2, sub_rows, dp_count, width_dev).transpose(0, 2, 1, 3)
    sums = lax.all_to_all(sums, "dp", split_axis=1, concat_axis=1, tiled=True)
    sums = sums.reshape(2, tok_rows, width_dev)
    return (
        sums[0],
        sums[1],
        weight_grads[None, :, :hidden],
        weight_grads[None, :, hidden : 2 * hidden],
        weight_grads[:, 2 * hidden :].T[None],
    )


def solution(mesh):
    placed = (
        P("expert", "dp"),
        P("expert", "dp"),
        P("expert", None),
        P("expert", None),
        P("expert", "dp", None),
        P("expert", "dp", None),
        P("expert", None, "dp"),
    )
    return jax.shard_map(
        shards,
        mesh=mesh,
        in_specs=placed,
        out_specs=(
            P("expert", "dp"),
            P("expert", "dp"),
            P("expert", "dp", None),
            P("expert", "dp", None),
            P("expert", None, "dp"),
        ),
        check_vma=False,
    )
```

time: 308 us -> 226 us (0.73)
  Pallas kernels: 208 us -> 141 us
  other arithmetic: 14.8 us -> 7.21 us
  local copies, waits for them, and re-layouts: 14.7 us -> 10.5 us
  matrix products: 27.9 us -> 23.9 us
    pallas_call x2, Pallas kernels: 208 us -> 141 us  [the longest x1 76.1 us: gather_rows(): pl.pallas_call(functools.partial(gather_kernel, side_z), out_shape=[jax.S...]
    concatenate x2 -> x1, other arithmetic: 8.26 us -> 0.01 us  [shards(): jnp.concatenate([both[1], extra], axis=1)]
    dot_general x6, matrix products: 27.9 us -> 23.9 us  [contract(): lax.dot_general(left_side, right_side, (((left_dim,), (right_dim,)), ((),...]
    unnamed x29, local copies, waits for them, and re-layouts: 12.5 us -> 8.81 us
  transfers between devices with their start and end apart: 3 -> 3, of which waited for: 1 -> 1; matrix products, arithmetic and copies ran while one was open for 8% -> 5% of each run, Pallas kernels for 68% -> 62%
where the time goes in v3:
time: 226 us
  Pallas kernels  141 us (62%)
  matrix products  23.9 us (11%)
  between operations  14.3 us (6%)
  blocking collectives  13.9 us (6%)
  local copies, waits for them, and re-layouts  10.5 us (5%)
  starting transfers between devices  10.2 us (5%)
  other arithmetic  7.21 us (3%)
  waiting for transfers between devices  4.91 us (2%)
    pallas_call x1, Pallas kernels, gather_rows(): pl.pallas_call(functools.partial(gather_kernel, side_z), out_shape=[jax.S...  76.1 us
    pallas_call x1, Pallas kernels, scatter_sums(): pl.pallas_call(functools.partial(scatter_kernel, side_z), out_shape=[jax....  64.9 us
    dot_general x6, matrix products, contract(): lax.dot_general(left_side, right_side, (((left_dim,), (right_dim,)), ((),...  23.9 us
    all_to_all x1, blocking collectives, shards(): sums = lax.all_to_all(sums, 'dp', split_axis=1, concat_axis=1, tiled=True)  13.9 us
    all_to_all x1, starting transfers between devices, shards(): both = lax.all_to_all(both, 'dp', split_axis=1, concat_axis=1, tiled=True)  10.1 us
    unnamed x29, local copies, waits for them, and re-layouts  8.81 us
    all_to_all x1, waiting for transfers between devices, shards(): both = lax.all_to_all(both, 'dp', split_axis=1, concat_axis=1, tiled=True)  4.86 us
  transfers between devices with their start and end apart: 3, of which 1 were waited for; matrix products, arithmetic and copies ran while one was open for 5% of the time, Pallas kernels for 62%

profile of v3, /device:TPU:1, one launch (start us, length us, event | category | flops | bytes accessed | tf_op | source)
XLA Modules:
  0.0 226.0 jit_solution(18108264320189540784)
XLA Ops:
  7.2 0.0 all-gather.2.cloned.1.call-start
  7.2 1.1 copy.48
  8.3 1.1 copy.49
  9.4 1.8 pad_maximum_fusion.4
  11.2 1.5 pad_maximum_fusion.5
  12.7 10.1 %all-to-all-start = ((bf16[2,8,16,256]{3,2,0,1:T(8,128)(2,1)}), bf16[2,8,16,256]{3,2,0,1:T(8,128)(2,1)S(1)}, u32[]{:S(2)}, u32[]{:S(2)}) async-start(bf16[2,8,16,256]{3,2,0,1:T(8,128)(2,1)} %pad_maximum_fusion.5), calls=%async_computation | async-start | bytes 262144 | tf_op jit(solution)/shard_map/all_to_all | solution.py:408
  22.9 0.1 constant_dynamic-slice_fusion
  22.9 0.1 copy.56
  23.0 0.1 constant_dynamic-slice_fusion.1
  23.1 0.1 copy.55
  23.2 0.1 fusion.25
  23.3 4.9 %all-to-all-done = bf16[2,8,16,256]{3,2,0,1:T(8,128)(2,1)S(1)} async-done(((bf16[2,8,16,256]{3,2,0,1:T(8,128)(2,1)}), bf16[2,8,16,256]{3,2,0,1:T(8,128)(2,1)S(1)}, u32[]{:S(2)}, u32[]{:S(2)}) %all-to-all-start) | async-done | bytes 131104 | tf_op jit(solution)/shard_map/all_to_all | solution.py:408
  28.2 76.1 %shard_map.110 = (bf16[4,16,16,2048]{3,2,1,0:T(8,128)(2,1)S(1)}, bf16[4,16,16,2176]{3,2,1,0:T(8,128)(2,1)S(1)}) custom-call(bf16[16,2048]{1,0:T(8,128)(2,1)S(1)} %bitcast.47, bf16[16,2176]{1,0:T(8,128)(2,1)S(1)} %pad_maximum_fusion.6.c_own), custom_call_target="tpu_custom_call" | custom-call | bytes 209715200 | tf_op jit(solution)/shard_map/pallas_call | solution.py:176
  104.3 2.0 copy-done.2
  106.4 2.1 copy-done.1
  108.5 0.1 copy.57
  108.7 0.0 all-gather.2.cloned.1.call-done
  108.7 6.3 %fusion.8 = f32[1024,768]{0,1:T(8,128)S(1)} fusion(bf16[1024,2048]{1,0:T(8,128)(2,1)} %bitcast.55, bf16[2048,1152]{0,1:T(8,128)(2,1)} %all-gather.2.cloned.1.call-done), kind=kOutput, calls=%fused_computation.10 | convolution fusion | flops 3221225472 | bytes 10485760 | tf_op jit(solution)/shard_map/dot_general | solution.py:12
  115.1 3.8 %multiply_convert_fusion.1 = (bf16[1024,384]{0,1:T(8,128)(2,1)S(1)}, bf16[1024,384]{0,1:T(8,128)(2,1)S(1)}, bf16[1024,384]{0,1:T(8,128)(2,1)S(1)}) fusion(f32[1024,768]{0,1:T(8,128)S(1)} %fusion.8, f32[1024]{0:T(1024)S(1)} %fusion.17, bf16[2048,1152]{0,1:T(8,128)(2,1)} %all-gather.2.cloned.1.call-done, bf16[1024,2176]{1,0:T(8,128)(2,1)S(1)} %bitcast.53), kind=kOutput, calls=%fused_computation.14 | convolution fusion | flops 1617297408 | bytes 11276288 | tf_op jit(solution)/shard_map/dot_general | solution.py:12
  118.9 1.8 fusion.4
  120.7 0.4 copy-done.3
  121.1 4.3 %convolution_convert_fusion.2 = bf16[2048,768]{0,1:T(8,128)(2,1)S(1)} fusion(bf16[1024,2048]{1,0:T(8,128)(2,1)S(1)} %bitcast.56, bf16[1024,384]{0,1:T(8,128)(2,1)S(1)} %get-tuple-element.34, bf16[1024,384]{0,1:T(8,128)(2,1)S(1)} %get-tuple-element.33), kind=kOutput, calls=%fused_computation.7 | convolution fusion | flops 3225944064 | bytes 8912896 | tf_op jit(solution)/shard_map/dot_general | solution.py:12
  125.3 2.6 %pad_maximum_fusion = bf16[2048,1152]{0,1:T(8,128)(2,1)} fusion(bf16[2048,384]{0,1:T(8,128)(2,1)S(1)} %fusion.4, bf16[2048,768]{0,1:T(8,128)(2,1)S(1)} %convolution_convert_fusion.2), kind=kLoop, calls=%fused_computation | loop fusion | flops 9437184 | bytes 9437184 | tf_op jit(solution)/shard_map/concatenate | solution.py:442
  127.9 4.0 %convolution_convert_fusion = bf16[1024,2048]{1,0:T(8,128)(2,1)S(1)} fusion(bf16[1024,384]{0,1:T(8,128)(2,1)S(1)} %get-tuple-element.35, bf16[2048,1152]{0,1:T(8,128)(2,1)} %all-gather.2.cloned.1.call-done), kind=kOutput, calls=%fused_computation.1 | convolution fusion | flops 1612709888 | bytes 6553600 | tf_op jit(solution)/shard_map/dot_general | solution.py:12
  131.9 3.8 %convolution_convert_fusion.1 = bf16[1024,2048]{1,0:T(8,128)(2,1)S(1)} fusion(bf16[2048,1152]{0,1:T(8,128)(2,1)S(1)} %bitcast.71, bf16[1024,384]{0,1:T(8,128)(2,1)S(1)} %get-tuple-element.34, bf16[1024,384]{0,1:T(8,128)(2,1)S(1)} %get-tuple-element.33), kind=kOutput, calls=%fused_computation.2 | convolution fusion | flops 3226468352 | bytes 8912896 | tf_op jit(solution)/shard_map/dot_general | solution.py:12
  135.7 64.9 %shard_map.111 = (bf16[16,2048]{1,0:T(8,128)(2,1)S(1)}, bf16[16,2048]{1,0:T(8,128)(2,1)S(1)}) custom-call(bf16[4,16,16,2048]{3,2,1,0:T(8,128)(2,1)S(1)} %bitcast.45, bf16[4,16,16,2048]{3,2,1,0:T(8,128)(2,1)S(1)} %bitcast.46), custom_call_target="tpu_custom_call" | custom-call | bytes 209715200 | tf_op jit(solution)/shard_map/pallas_call | solution.py:361
  200.7 13.9 %all_to_all.10 = bf16[2,8,16,256]{3,2,0,1:T(8,128)(2,1)S(1)} all-to-all(bf16[2,8,16,256]{3,2,0,1:T(8,128)(2,1)S(1)} %maximum_bitcast_fusion), channel_id=1, replica_groups=mesh['dp'=8,'expert'=64] {'dp'}, dimensions={1} | all-to-all | bytes 262144 | tf_op jit(solution)/shard_map/all_to_all | solution.py:446
  214.7 0.7 fusion.28
  215.3 1.1 convert_element_type.62
  216.5 0.8 slice_bitcast_fusion
  217.3 0.9 copy.54
  218.2 0.9 copy.53
  (35 shorter events, 0.2 us)
Async XLA Ops:
  7.2 15.7 %copy-start = (f32[128,8]{0,1:T(8,128)S(1)}, f32[128,8]{0,1:T(8,128)}, u32[]{:S(2)}) copy-start(f32[128,8]{0,1:T(8,128)} %param.10) | copy-start | bytes 12292
  7.2 15.8 %copy-start.4 = (s32[128,8]{0,1:T(8,128)S(1)}, s32[128,8]{0,1:T(8,128)}, u32[]{:S(2)}) copy-start(s32[128,8]{0,1:T(8,128)} %param.9) | copy-start | bytes 12292
  7.2 101.5 %all-gather.2.cloned.1.call-start = ((), (), s32[]{:S(2)}) async-start(), calls=%async_computation.3 | async-start | bytes 5308416 | tf_op jit(solution)/shard_map/all_gather | solution.py:405
  12.7 15.4 %all-to-all-start = ((bf16[2,8,16,256]{3,2,0,1:T(8,128)(2,1)}), bf16[2,8,16,256]{3,2,0,1:T(8,128)(2,1)S(1)}, u32[]{:S(2)}, u32[]{:S(2)}) async-start(bf16[2,8,16,256]{3,2,0,1:T(8,128)(2,1)} %pad_maximum_fusion.5), calls=%async_computation | async-start | bytes 262144 | tf_op jit(solution)/shard_map/all_to_all | solution.py:408
  22.9 192.5 %reduce-scatter.2.cloned.1.call-start = ((), (), s32[]{:S(2)}) async-start(), calls=%async_computation.4 | async-start | bytes 5308416 | tf_op jit(solution)/shard_map/reduce_scatter | solution.py:441
  104.3 2.1 copy-start.2
  106.4 2.1 copy-start.1
  108.6 6.5 %slice-start = ((s8[4456448]{0:T(1024)(128)(4,1)}), s8[262144]{0:T(1024)(128)(4,1)S(1)}, s32[]{:S(2)}) async-start(s8[4456448]{0:T(1024)(128)(4,1)} %bitcast.51), calls=%async_computation.5 | async-start | bytes 524288
  108.7 6.4 %slice-start.1 = ((s8[4456448]{0:T(1024)(128)(4,1)}), s8[4194304]{0:T(1024)(128)(4,1)S(1)}, s32[]{:S(2)}) async-start(s8[4456448]{0:T(1024)(128)(4,1)} %bitcast.51), calls=%async_computation.6 | async-start | bytes 8388608
  118.9 2.2 copy-start.3
  127.9 4.0 %slice-start.2 = ((s8[4718592]{0:T(1024)(128)(4,1)}), s8[524288]{0:T(1024)(128)(4,1)S(1)}, s32[]{:S(2)}) async-start(s8[4718592]{0:T(1024)(128)(4,1)} %bitcast.70), calls=%async_computation.7 | async-start | bytes 1048576
  127.9 4.0 %slice-start.3 = ((s8[4718592]{0:T(1024)(128)(4,1)}), s8[4194304]{0:T(1024)(128)(4,1)S(1)}, s32[]{:S(2)}) async-start(s8[4718592]{0:T(1024)(128)(4,1)} %bitcast.70), calls=%async_computation.8 | async-start | bytes 8388608
Sparse Core Ops, SparseCore 0:
  11.3 51.0 all-gather.1
  128.0 41.4 reduce-scatter.1

commit v4 on v3

--- a/solution.py
+++ b/solution.py
@@ -77,21 +77,53 @@
     return lax.rem(value + 2 * count, count)
 
 
-def gather_kernel(side_z, x_own, c_own, x_all, c_all, xz_send, xz_recv, xy_send, xy_recv,
-                  cy_send, cy_recv, cz_send, cz_recv, own_sem):
+def dp_places(dp_count):
+    me = lax.axis_index("dp")
+    others = [lax.rem(me + hop, dp_count) for hop in range(1, dp_count)]
+    return (me, others, [{"dp": other} for other in others])
+
+
+def part_of(index, size):
+    return pl.ds(pl.multiple_of(index * size, size), size)
+
+
+def gather_kernel(side_z, dp_count, tok_ref, cot_ref, extra_ref, x_all, c_all, xz_send,
+                  xz_recv, xy_send, xy_recv, cy_send, cy_recv, cz_send, cz_recv,
+                  dp_send, dp_recv, own_sem):
     y_at, z_at, along_y, along_z = ring_places(side_z)
+    me, others, other_places = dp_places(dp_count)
+    width_dev = tok_ref.shape[1]
+    rows = tok_ref.shape[0] // dp_count
+    mine = part_of(me, rows)
+    columns = part_of(me, width_dev)
+    width = pl.ds(dp_count * width_dev, extra_ref.shape[1])
+    pairs = ((tok_ref, x_all), (cot_ref, c_all))
     own_copies = [
-        pltpu.make_async_copy(x_own, x_all.at[y_at, z_at], own_sem.at[0]),
-        pltpu.make_async_copy(c_own, c_all.at[y_at, z_at], own_sem.at[1]),
+        pltpu.make_async_copy(held.at[mine], whole.at[y_at, z_at, :, columns], own_sem.at[i])
+        for i, (held, whole) in enumerate(pairs)
     ]
+    own_copies.append(
+        pltpu.make_async_copy(extra_ref, c_all.at[y_at, z_at, :, width], own_sem.at[2])
+    )
     for copy in own_copies:
         copy.start()
-    greet([along_y(1), along_y(-1), along_z(1), along_z(-1)])
+    greet([along_y(1), along_y(-1), along_z(1), along_z(-1)] + other_places)
+    swapped = []
+    for i, (held, whole) in enumerate(pairs):
+        for hop, (other, place) in enumerate(zip(others, other_places)):
+            swapped.append(send(
+                held.at[part_of(other, rows)],
+                whole.at[y_at, z_at, :, columns],
+                (dp_send.at[i, hop], dp_recv.at[i, hop]),
+                place,
+            ))
     for copy in own_copies:
         copy.wait()
+    for copy in swapped:
+        copy.wait_recv()
     step_counts = steps_of(side_z)
-    span = SIDE_Y // PIECES
     up_y, down_y = wrap(y_at - 1, SIDE_Y), wrap(y_at + 1, SIDE_Y)
+    held_rows = (y_at, up_y, down_y, wrap(y_at + 2, SIDE_Y))
     xz, xy, cz = {}, {}, {}
 
     def start_xz(way, step):
@@ -105,32 +137,35 @@
         return wrap(z_at - sign * ((number + 1) // 2), side_z)
 
     def start_xy(number, hop):
-        row = up_y if hop == 2 else y_at
+        down = number % 2 if hop == 2 else hop
+        row = (up_y, down_y)[down] if hop == 2 else y_at
         block = x_all.at[row, place_of(number)]
         at = (number, hop)
         xy[at] = send(
-            block, block, (xy_send.at[at], xy_recv.at[at]), along_y(-1 if hop == 1 else 1)
+            block, block, (xy_send.at[at], xy_recv.at[at]), along_y(1 - 2 * down)
         )
 
     def start_cz(way, step, piece):
         sign = 1 - 2 * way
-        block = c_all.at[pl.ds(piece * span, span), wrap(z_at - sign * step, side_z)]
+        block = c_all.at[held_rows[piece], wrap(z_at - sign * step, side_z)]
         at = (way, step, piece)
         cz[at] = send(block, block, (cz_send.at[at], cz_recv.at[at]), along_z(sign))
 
     start_xz(0, 0)
     start_xz(1, 0)
-    mine = c_all.at[y_at, z_at]
-    first = send(mine, mine, (cy_send.at[0], cy_recv.at[0]), along_y(1))
-    other = send(mine, mine, (cy_send.at[1], cy_recv.at[1]), along_y(-1))
+    block = c_all.at[y_at, z_at]
+    first = send(block, block, (cy_send.at[0], cy_recv.at[0]), along_y(1))
+    other = send(block, block, (cy_send.at[1], cy_recv.at[1]), along_y(-1))
+    for way in range(2):
+        start_cz(way, 0, 0)
     start_xy(0, 0)
     start_xy(0, 1)
     first.wait_recv()
     below = c_all.at[up_y, z_at]
     second = send(below, below, (cy_send.at[2], cy_recv.at[2]), along_y(1))
-    other.wait_recv()
-    second.wait_recv()
-    for piece in range(PIECES):
+    for piece, copy in ((1, None), (2, other), (3, second)):
+        if copy is not None:
+            copy.wait_recv()
         for way in range(2):
             start_cz(way, 0, piece)
     passed = 0
@@ -146,40 +181,41 @@
                 start_xy(2 * step + 1 + way, 1)
                 arrived += 1
         for number in range(passed, ready):
-            xy[(number, 0)].wait_recv()
+            xy[(number, number % 2)].wait_recv()
             start_xy(number, 2)
         passed = ready
-        for piece in range(PIECES):
+        for piece in range(SIDE_Y):
             for way in range(2):
                 if step < step_counts[way]:
                     cz[(way, step, piece)].wait_recv()
                     if step + 1 < step_counts[way]:
                         start_cz(way, step + 1, piece)
     for number in range(passed, side_z):
-        xy[(number, 0)].wait_recv()
+        xy[(number, number % 2)].wait_recv()
         start_xy(number, 2)
     for number in range(side_z):
-        xy[(number, 1)].wait_recv()
+        xy[(number, 1 - number % 2)].wait_recv()
         xy[(number, 2)].wait_recv()
     for group in (xz, xy, cz):
         for copy in group.values():
             copy.wait_send()
-    for copy in (first, other, second):
+    for copy in (first, other, second, *swapped):
         copy.wait_send()
 
 
-def gather_rows(x_own, c_own, side_z):
-    rows = x_own.shape[0]
+def gather_rows(tokens, cotangent, extra, side_z, dp_count):
+    rows = extra.shape[0]
+    width = tokens.shape[1] * dp_count
     longest = steps_of(side_z)[0]
     vmem = pl.BlockSpec(memory_space=pltpu.VMEM)
     sem = pltpu.SemaphoreType.DMA
     gathered = pl.pallas_call(
-        functools.partial(gather_kernel, side_z),
+        functools.partial(gather_kernel, side_z, dp_count),
         out_shape=[
-            jax.ShapeDtypeStruct((SIDE_Y, side_z, *own.shape), own.dtype)
-            for own in (x_own, c_own)
+            jax.ShapeDtypeStruct((SIDE_Y, side_z, rows, columns), tokens.dtype)
+            for columns in (width, width + extra.shape[1])
         ],
-        in_specs=[vmem, vmem],
+        in_specs=[vmem, vmem, vmem],
         out_specs=[vmem, vmem],
         scratch_shapes=[
             sem((2, longest)),
@@ -188,25 +224,46 @@
             sem((side_z, 3)),
             sem((3,)),
             sem((3,)),
-            sem((2, longest, PIECES)),
-            sem((2, longest, PIECES)),
-            sem((2,)),
+            sem((2, longest, SIDE_Y)),
+            sem((2, longest, SIDE_Y)),
+            sem((2, dp_count - 1)),
+            sem((2, dp_count - 1)),
+            sem((3,)),
         ],
         compiler_params=pltpu.CompilerParams(
-            collective_id=0, has_side_effects=True, vmem_limit_bytes=24 * 2**20
+            collective_id=0, has_side_effects=True, vmem_limit_bytes=14 * 2**20
         ),
         cost_estimate=pl.CostEstimate(
             flops=0, bytes_accessed=200 * 2**20, transcendentals=0
         ),
-    )(x_own, c_own)
+    )(tokens, cotangent, extra)
     return [whole.reshape(SIDE_Y * side_z * rows, -1) for whole in gathered]
 
 
-def scatter_kernel(side_z, m_part, g_part, m_sum, g_sum, m_up, m_down, m_held, m_got,
+def scatter_kernel(side_z, dp_count, m_part, g_part, m_out, g_out, m_sum, g_sum, m_up, m_down, m_held, m_got,
                    g_y, g_held, g_up, g_down, mz_send, mz_recv, my_send, my_recv,
-                   gy_send, gy_recv, gz_send, gz_recv):
+                   gy_send, gy_recv, gz_send, gz_recv, dp_send, dp_recv, own_sem):
     y_at, z_at, along_y, along_z = ring_places(side_z)
-    greet([along_y(1), along_y(-1), along_z(1), along_z(-1)])
+    me, others, other_places = dp_places(dp_count)
+    greet([along_y(1), along_y(-1), along_z(1), along_z(-1)] + other_places)
+    width_dev = m_out.shape[1]
+    mine = part_of(me, m_out.shape[0] // dp_count)
+    columns = part_of(me, width_dev)
+    own_copies, swapped = [], []
+
+    def hand_out(i, total, result):
+        own_copies.append(
+            pltpu.make_async_copy(total.at[:, columns], result.at[mine], own_sem.at[i])
+        )
+        own_copies[-1].start()
+        for hop, (other, place) in enumerate(zip(others, other_places)):
+            swapped.append(send(
+                total.at[:, part_of(other, width_dev)],
+                result.at[mine],
+                (dp_send.at[i, hop], dp_recv.at[i, hop]),
+                place,
+            ))
+
     step_counts = steps_of(side_z)
     span = SIDE_Y // PIECES
     half = side_z // 2
@@ -338,19 +395,25 @@
     down.wait_recv()
     near.wait_recv()
     m_sum[...] = rounded_sum(m_held[y_at], m_got[1], m_got[2])
+    hand_out(0, m_sum, m_out)
     for way in range(2):
         gz[(way, step_counts[way] - 1)].wait_recv()
     g_sum[...] = rounded_sum(
         g_held[z_at], g_up[step_counts[0] - 1], g_down[step_counts[1] - 1]
     )
+    hand_out(1, g_sum, g_out)
+    for copy in own_copies:
+        copy.wait()
+    for copy in swapped:
+        copy.wait_recv()
     for group in (mz, gz, gy):
         for copy in group.values():
             copy.wait_send()
-    for copy in (far, down, near):
+    for copy in (far, down, near, *swapped):
         copy.wait_send()
 
 
-def scatter_sums(m_part, g_part, side_z):
+def scatter_sums(m_part, g_part, side_z, dp_count):
     all_rows, columns = m_part.shape
     rows = all_rows // (SIDE_Y * side_z)
     up_steps, down_steps = steps_of(side_z)
@@ -359,11 +422,13 @@
     sem = pltpu.SemaphoreType.DMA
     whole = (SIDE_Y, side_z, rows, columns)
     return pl.pallas_call(
-        functools.partial(scatter_kernel, side_z),
-        out_shape=[jax.ShapeDtypeStruct((rows, columns), kind)] * 2,
+        functools.partial(scatter_kernel, side_z, dp_count),
+        out_shape=[jax.ShapeDtypeStruct((rows * dp_count, columns // dp_count), kind)] * 2,
         in_specs=[vmem, vmem],
         out_specs=[vmem, vmem],
         scratch_shapes=[
+            pltpu.VMEM((rows, columns), kind),
+            pltpu.VMEM((rows, columns), kind),
             pltpu.VMEM((up_steps, SIDE_Y, rows, columns), kind),
             pltpu.VMEM((down_steps, SIDE_Y, rows, columns), kind),
             pltpu.VMEM((SIDE_Y, rows, columns), kind),
@@ -380,9 +445,12 @@
             sem((6,)),
             sem((2, up_steps)),
             sem((2, up_steps)),
+            sem((2, dp_count - 1)),
+            sem((2, dp_count - 1)),
+            sem((2,)),
         ],
         compiler_params=pltpu.CompilerParams(
-            collective_id=1, has_side_effects=True, vmem_limit_bytes=32 * 2**20
+            collective_id=1, has_side_effects=True, vmem_limit_bytes=24 * 2**20
         ),
         cost_estimate=pl.CostEstimate(
             flops=0, bytes_accessed=200 * 2**20, transcendentals=0
@@ -404,9 +472,6 @@
     weights_dev = jnp.concatenate([w_gate[0], w_up[0], w_down[0].T], axis=1)
     weights = lax.all_gather(weights_dev, "dp", axis=0, tiled=True)
 
-    both = jnp.stack([tokens, cotangent]).reshape(2, dp_count, sub_rows, width_dev)
-    both = lax.all_to_all(both, "dp", split_axis=1, concat_axis=1, tiled=True)
-    both = both.transpose(0, 2, 1, 3).reshape(2, sub_rows, width)
     my_routes = lax.dynamic_slice_in_dim(routes, me_dp * sub_rows, sub_rows, 0)
     my_mix = lax.dynamic_slice_in_dim(mix_weights, me_dp * sub_rows, sub_rows, 0)
     extra = jnp.concatenate(
@@ -414,7 +479,7 @@
     )
     extra = jnp.pad(extra, ((0, 0), (0, 128 - extra.shape[1])))
     x_rows, c_wide = gather_rows(
-        both[0], jnp.concatenate([both[1], extra], axis=1), owner_count // SIDE_Y
+        tokens, cotangent, extra, owner_count // SIDE_Y, dp_count
     )
     c_rows = c_wide[:, :width]
     tail = c_wide[:, width : width + 4 * picks_per].astype(jnp.float32)
@@ -441,13 +506,10 @@
     weight_grads = lax.psum_scatter(
         jnp.concatenate([in_grad, out_grad], axis=1), "dp", scatter_dimension=0, tiled=True
     ).astype(jnp.float32)
-    sums = jnp.stack(scatter_sums(mixed_part, grad_part, owner_count // SIDE_Y))
-    sums = sums.reshape(2, sub_rows, dp_count, width_dev).transpose(0, 2, 1, 3)
-    sums = lax.all_to_all(sums, "dp", split_axis=1, concat_axis=1, tiled=True)
-    sums = sums.reshape(2, tok_rows, width_dev)
+    mixed, token_grad = scatter_sums(mixed_part, grad_part, owner_count // SIDE_Y, dp_count)
     return (
-        sums[0],
-        sums[1],
+        mixed,
+        token_grad,
         weight_grads[None, :, :hidden],
         weight_grads[None, :, hidden : 2 * hidden],
         weight_grads[:, 2 * hidden :].T[None],

time: 226 us -> 221 us (0.978)
  Pallas kernels: 141 us -> 163 us
  blocking collectives: 13.9 us -> 0 us
  starting transfers between devices: 10.2 us -> 0.08 us
  waiting for transfers between devices: 4.91 us -> 0.08 us
  local copies, waits for them, and re-layouts: 10.5 us -> 13.4 us
    pallas_call x2, Pallas kernels: 141 us -> 163 us  [the longest x1 83.2 us: gather_rows(): pl.pallas_call(functools.partial(gather_kernel, side_z, dp_count), out_sh...]
    all_to_all x1 -> x0, blocking collectives: 13.9 us -> none  [shards(): sums = lax.all_to_all(sums, 'dp', split_axis=1, concat_axis=1, tiled=True)]
    all_to_all x1 -> x0, starting transfers between devices: 10.1 us -> none  [shards(): both = lax.all_to_all(both, 'dp', split_axis=1, concat_axis=1, tiled=True)]
    all_to_all x1 -> x0, waiting for transfers between devices: 4.86 us -> none  [shards(): both = lax.all_to_all(both, 'dp', split_axis=1, concat_axis=1, tiled=True)]
    unnamed x29, local copies, waits for them, and re-layouts: 8.81 us -> 11.7 us
  transfers between devices with their start and end apart: 3 -> 2, of which waited for: 1 -> 0; matrix products, arithmetic and copies ran while one was open for 5% -> 4% of each run, Pallas kernels for 62% -> 74%
where the time goes in v4:
time: 221 us; the launch traced here: 220 us
  Pallas kernels  163 us (74%)
  matrix products  24.1 us (11%)
  between operations  14.3 us (6%)
  local copies, waits for them, and re-layouts  13.4 us (6%)
  other arithmetic  5.61 us (3%)
    pallas_call x1, Pallas kernels, gather_rows(): pl.pallas_call(functools.partial(gather_kernel, side_z, dp_count), out_sh...  83.2 us
    pallas_call x1, Pallas kernels, scatter_sums(): pl.pallas_call(functools.partial(scatter_kernel, side_z, dp_count), out_s...  79.4 us
    dot_general x6, matrix products, contract(): lax.dot_general(left_side, right_side, (((left_dim,), (right_dim,)), ((),...  24.1 us
    unnamed x29, local copies, waits for them, and re-layouts  11.7 us
  transfers between devices with their start and end apart: 2, of which 0 were waited for; matrix products, arithmetic and copies ran while one was open for 4% of the time, Pallas kernels for 74%

profile of v4, /device:TPU:1, one launch (start us, length us, event | category | flops | bytes accessed | tf_op | source)
XLA Modules:
  0.0 220.1 jit_solution(16678845068462525517)
XLA Ops:
  7.2 0.0 all-gather.2.cloned.1.call-start
  7.2 1.1 copy.27
  8.3 1.1 copy.28
  9.4 1.8 pad_maximum_fusion.4
  11.2 0.0 reduce-scatter.2.cloned.1.call-start
  11.2 0.1 constant_dynamic-slice_fusion
  11.3 0.1 copy.33
  11.4 0.8 constant_dynamic-slice_fusion.1
  12.1 0.1 copy.32
  12.2 0.1 fusion.25.extra_ref
  12.3 0.8 copy-done.1
  13.2 0.8 copy-done.2
  14.0 83.2 %shard_map.110 = (bf16[4,16,16,2048]{3,2,1,0:T(8,128)(2,1)S(1)}, bf16[4,16,16,2176]{3,2,1,0:T(8,128)(2,1)S(1)}) custom-call(bf16[128,256]{1,0:T(8,128)(2,1)S(1)} %copy-done.1, bf16[128,256]{1,0:T(8,128)(2,1)S(1)} %copy-done.2, bf16[16,128]{1,0:T(8,128)(2,1)S(1)} %fusion.25.extra_ref), custom_call_target="tpu_custom_call" | custom-call | bytes 209715200 | tf_op jit(solution)/shard_map/pallas_call | solution.py:212
  97.2 2.1 copy-done.4
  99.3 2.1 copy-done.3
  101.4 0.1 copy.34
  101.6 0.0 all-gather.2.cloned.1.call-done
  101.6 6.3 %fusion.8 = f32[1024,768]{0,1:T(8,128)S(1)} fusion(bf16[1024,2048]{1,0:T(8,128)(2,1)} %bitcast.31, bf16[2048,1152]{0,1:T(8,128)(2,1)} %all-gather.2.cloned.1.call-done), kind=kOutput, calls=%fused_computation.10 | convolution fusion | flops 3221225472 | bytes 10485760 | tf_op jit(solution)/shard_map/dot_general | solution.py:12
  108.0 3.8 %multiply_convert_fusion.1 = (bf16[1024,384]{0,1:T(8,128)(2,1)S(1)}, bf16[1024,384]{0,1:T(8,128)(2,1)S(1)}, bf16[1024,384]{0,1:T(8,128)(2,1)S(1)}) fusion(f32[1024,768]{0,1:T(8,128)S(1)} %fusion.8, f32[1024]{0:T(1024)S(1)} %fusion.17, bf16[2048,1152]{0,1:T(8,128)(2,1)} %all-gather.2.cloned.1.call-done, bf16[1024,2176]{1,0:T(8,128)(2,1)S(1)} %bitcast.29), kind=kOutput, calls=%fused_computation.14 | convolution fusion | flops 1617297408 | bytes 11276288 | tf_op jit(solution)/shard_map/dot_general | solution.py:12
  111.8 1.8 fusion.4
  113.6 0.4 copy-done.5
  114.0 4.3 %convolution_convert_fusion.2 = bf16[2048,768]{0,1:T(8,128)(2,1)S(1)} fusion(bf16[1024,2048]{1,0:T(8,128)(2,1)S(1)} %bitcast.32, bf16[1024,384]{0,1:T(8,128)(2,1)S(1)} %get-tuple-element.29, bf16[1024,384]{0,1:T(8,128)(2,1)S(1)} %get-tuple-element.28), kind=kOutput, calls=%fused_computation.7 | convolution fusion | flops 3225944064 | bytes 8912896 | tf_op jit(solution)/shard_map/dot_general | solution.py:12
  118.3 2.6 %pad_maximum_fusion = bf16[2048,1152]{0,1:T(8,128)(2,1)} fusion(bf16[2048,384]{0,1:T(8,128)(2,1)S(1)} %fusion.4, bf16[2048,768]{0,1:T(8,128)(2,1)S(1)} %convolution_convert_fusion.2), kind=kLoop, calls=%fused_computation | loop fusion | flops 9437184 | bytes 9437184 | tf_op jit(solution)/shard_map/concatenate | solution.py:507
  120.9 4.0 %convolution_convert_fusion = bf16[1024,2048]{1,0:T(8,128)(2,1)S(1)} fusion(bf16[1024,384]{0,1:T(8,128)(2,1)S(1)} %get-tuple-element.30, bf16[2048,1152]{0,1:T(8,128)(2,1)} %all-gather.2.cloned.1.call-done), kind=kOutput, calls=%fused_computation.1 | convolution fusion | flops 1612709888 | bytes 6553600 | tf_op jit(solution)/shard_map/dot_general | solution.py:12
  124.9 3.9 %convolution_convert_fusion.1 = bf16[1024,2048]{1,0:T(8,128)(2,1)S(1)} fusion(bf16[2048,1152]{0,1:T(8,128)(2,1)S(1)} %bitcast.37, bf16[1024,384]{0,1:T(8,128)(2,1)S(1)} %get-tuple-element.29, bf16[1024,384]{0,1:T(8,128)(2,1)S(1)} %get-tuple-element.28), kind=kOutput, calls=%fused_computation.2 | convolution fusion | flops 3226468352 | bytes 8912896 | tf_op jit(solution)/shard_map/dot_general | solution.py:12
  128.8 79.4 %shard_map.111 = (bf16[128,256]{1,0:T(8,128)(2,1)S(1)}, bf16[128,256]{1,0:T(8,128)(2,1)S(1)}) custom-call(bf16[4,16,16,2048]{3,2,1,0:T(8,128)(2,1)S(1)} %bitcast.24, bf16[4,16,16,2048]{3,2,1,0:T(8,128)(2,1)S(1)} %bitcast.25), custom_call_target="tpu_custom_call" | custom-call | bytes 209715200 | tf_op jit(solution)/shard_map/pallas_call | solution.py:424
  208.2 1.1 convert_element_type.62
  209.4 0.8 slice_bitcast_fusion
  210.2 0.9 copy.31
  211.1 0.9 copy.30
  212.0 0.6 copy.37
  212.7 0.6 copy.38
  (25 shorter events, 0.2 us)
Async XLA Ops:
  7.2 4.1 %copy-start = (f32[128,8]{0,1:T(8,128)S(1)}, f32[128,8]{0,1:T(8,128)}, u32[]{:S(2)}) copy-start(f32[128,8]{0,1:T(8,128)} %param.10) | copy-start | bytes 12292
  7.2 94.4 %all-gather.2.cloned.1.call-start = ((), (), s32[]{:S(2)}) async-start(), calls=%async_computation.1 | async-start | bytes 5308416 | tf_op jit(solution)/shard_map/all_gather | solution.py:473
  11.2 197.1 %reduce-scatter.2.cloned.1.call-start = ((), (), s32[]{:S(2)}) async-start(), calls=%async_computation.2 | async-start | bytes 5308416 | tf_op jit(solution)/shard_map/reduce_scatter | solution.py:506
  12.3 0.8 copy-start.1
  13.1 0.8 copy-start.2
  97.2 2.1 copy-start.4
  99.3 2.1 copy-start.3
  101.5 6.5 %slice-start = ((s8[4456448]{0:T(1024)(128)(4,1)}), s8[262144]{0:T(1024)(128)(4,1)S(1)}, s32[]{:S(2)}) async-start(s8[4456448]{0:T(1024)(128)(4,1)} %bitcast.27), calls=%async_computation.3 | async-start | bytes 524288
  101.6 6.4 %slice-start.1 = ((s8[4456448]{0:T(1024)(128)(4,1)}), s8[4194304]{0:T(1024)(128)(4,1)S(1)}, s32[]{:S(2)}) async-start(s8[4456448]{0:T(1024)(128)(4,1)} %bitcast.27), calls=%async_computation.4 | async-start | bytes 8388608
  111.8 2.2 copy-start.5
  120.8 4.0 %slice-start.2 = ((s8[4718592]{0:T(1024)(128)(4,1)}), s8[524288]{0:T(1024)(128)(4,1)S(1)}, s32[]{:S(2)}) async-start(s8[4718592]{0:T(1024)(128)(4,1)} %bitcast.36), calls=%async_computation.5 | async-start | bytes 1048576
  120.9 4.0 %slice-start.3 = ((s8[4718592]{0:T(1024)(128)(4,1)}), s8[4194304]{0:T(1024)(128)(4,1)S(1)}, s32[]{:S(2)}) async-start(s8[4718592]{0:T(1024)(128)(4,1)} %bitcast.36), calls=%async_computation.6 | async-start | bytes 8388608
Sparse Core Ops, SparseCore 0:
  11.3 51.0 all-gather.1
  121.0 41.7 reduce-scatter.1
